TPU v7x, 256 devices: a whole 4x4x8 slice. The times are simulated.
256 devices in a mesh: expert: 32 (over z, y), vocab: 8 (over x, core).
Axes of the slice: x: 4, y: 4, z: 8, core: 2. Of those that a mesh axis runs over, the one named last changes fastest.
Arguments:
- tokens: bfloat16 [8192, 2048], P('expert'), may hold values from -6 to 6
- teacher_expert: int32 [8192, 1], P('expert'), may hold values from 0 to 15
- student_expert: int32 [8192, 1], P('expert'), may hold values from 0 to 15
- priority: int32 [32, 256], P('expert'), may hold values from 0 to 255, each once within a row
- expert_in: bfloat16 [32, 2048, 8192], P('expert', None, 'vocab'), may hold values from -0.125 to 0.125
- expert_out: bfloat16 [32, 8192, 2048], P('expert', 'vocab'), may hold values from -0.0625 to 0.0625
- teacher_gain: float32 [2048], replicated, may hold values from 0.1 to 1.9
- student_gain: float32 [2048], replicated, may hold values from 0.1 to 1.9
- teacher_head: bfloat16 [16384, 2048], P(('vocab', 'expert')), may hold values from -4 to 4
- student_head: bfloat16 [16384, 2048], P(('vocab', 'expert')), may hold values from -4 to 4
Outputs:
- token_kl: float32 [8192], P('expert')
Inputs may be any that keep to these rules, and one draw needn't show every extreme that they name: Each row of priority holds every number of 0 to 255 once.
All inputs are finite; a program needn't handle non-finite values.
Results may differ from a plain program's by a relative error of at most 0.0032.
Values may be sent and summed in bfloat16 or wider, within the bound.
A program may use at most 128 MiB of HBM per device.

v0:
```python
import jax
import jax.numpy as jnp
from jax import lax
from jax.sharding import Mesh
from jax.sharding import PartitionSpec as P

VOCAB = ("vocab_0", "vocab_1")
VOCAB_EXPERT = ("vocab_0", "vocab_1", "expert")


def cut_along(array, dim, count):
    shape = array.shape
    blocks = array.reshape(*shape[:dim], count, shape[dim] // count, *shape[dim + 1 :])
    return jnp.moveaxis(blocks, dim, 0)


def sum_at_owner(array, axis, dim):
    blocks = cut_along(array, dim, lax.axis_size(axis))
    arrived = lax.all_to_all(blocks, axis, split_axis=0, concat_axis=0, tiled=True)
    return arrived.sum(axis=0)


def sum_in_two_steps(array, axes, dim):
    far, near = axes
    blocks = cut_along(array, dim, lax.axis_size(far))
    nearer = sum_at_owner(blocks, near, dim + 1)
    arrived = lax.all_to_all(nearer, far, split_axis=0, concat_axis=0, tiled=True)
    return arrived.sum(axis=0)


def copy_for_each(array, axis):
    count = lax.axis_size(axis)
    return lax.all_to_all(
        jnp.broadcast_to(array[None], (count, *array.shape)), axis, 0, 0, tiled=True
    )


def in_order(blocks, dim):
    shape = list(blocks.shape[1:])
    shape[dim] *= blocks.shape[0]
    return jnp.moveaxis(blocks, 0, dim).reshape(shape)


def gather_axes(array, axes, dim):
    far, near = axes
    initial = copy_for_each(array, far)
    blocks = jnp.swapaxes(copy_for_each(initial, near), 0, 1)
    return in_order(blocks.reshape(-1, *array.shape), dim)


def side_by_side(arrays, axis, dim, along):
    widths = [a.shape[along] for a in arrays]
    both = jnp.concatenate(arrays, axis=along)
    filled = gather_axes(both, axis, dim)
    return tuple(jnp.split(filled, [sum(widths[:k]) for k in range(1, len(widths))], axis=along))


def sent_together(arrays, axis, dim, along):
    ends, at = ([], 0)
    for a in arrays[:-1]:
        at += a.shape[along]
        ends.append(at)
    both = jnp.concatenate(arrays, axis=along)
    return tuple(jnp.split(lax.all_gather(both, axis, axis=dim, tiled=True), ends, axis=along))


def all_in_one(array, axis):
    leaves = jax.tree.leaves(array)
    sequence = sorted(range(len(leaves)), key=lambda k: -leaves[k].size)
    width = (1, *leaves[sequence[0]].shape)[-1]
    lines = [
        jnp.pad(leaves[k].reshape(-1), (0, -leaves[k].size % width)).reshape(-1, width)
        for k in sequence
    ]
    both, at, found = (copy_for_each(jnp.concatenate(lines), axis), 0, {})
    for k, line in zip(sequence, lines):
        slab = both[:, at : at + len(line)].reshape(len(both), -1)
        found[k] = slab[:, : leaves[k].size].reshape(-1, *leaves[k].shape)
        at += len(line)
    numbers = iter(range(len(leaves)))
    return jax.tree.map(lambda _: found[next(numbers)], array)


def combined_pairwise(pieces, combine):
    while len(jax.tree.leaves(pieces)[0]) > 1:
        pieces = jax.vmap(combine)(
            *(jax.tree.map(lambda part: part[side::2], pieces) for side in (0, 1))
        )
    return jax.tree.map(lambda part: part[0], pieces)


def combined_all(array, axis, combine):
    pieces = all_in_one(array, axis)
    return combined_pairwise(pieces, combine)


def slot_places(expert, ranking, capacity, lane, dump):
    same_expert = expert[:, None] == expert[None, :]
    before = ranking[None, :] < ranking[:, None]
    slot_rank = jnp.sum(jnp.logical_and(same_expert, before).astype(jnp.int32), axis=1)
    kept_mask = slot_rank < capacity
    return jnp.where(kept_mask, (2 * expert + lane) * capacity + slot_rank, dump)


def normed(tokens, branch, gain_vector):
    summed = tokens.astype(jnp.float32) + branch.astype(jnp.float32)
    factor = lax.rsqrt(jnp.mean(summed * summed, axis=-1, keepdims=True) + 1e-05)
    return (summed * factor * gain_vector).astype(jnp.bfloat16)


def combine_stats(first, second):
    teacher_peak = jnp.maximum(first[0], second[0])
    student_peak = jnp.maximum(first[2], second[2])
    first_teacher = jnp.exp(first[0] - teacher_peak)
    second_teacher = jnp.exp(second[0] - teacher_peak)
    first_student = jnp.exp(first[2] - student_peak)
    second_student = jnp.exp(second[2] - student_peak)
    return (
        teacher_peak,
        first[1] * first_teacher + second[1] * second_teacher,
        student_peak,
        first[3] * first_student + second[3] * second_student,
        first[4] * first_teacher + second[4] * second_teacher,
    )


def local(
    tokens,
    teacher_expert,
    student_expert,
    priority,
    expert_in,
    expert_out,
    teacher_gain,
    student_gain,
    teacher_head,
    student_head,
):
    count, width = tokens.shape
    experts = lax.axis_size("expert")
    shards = lax.axis_size(VOCAB)
    capacity = 3 * count // experts
    dump = experts * capacity
    ranking = priority[0]
    teacher_places = slot_places(teacher_expert[:, 0], ranking, capacity, 0, dump)
    student_places = slot_places(student_expert[:, 0], ranking, capacity, 1, dump)
    numbers = jnp.arange(count, dtype=jnp.int32)
    owners = (
        jnp.full((dump + 1,), count, jnp.int32)
        .at[teacher_places]
        .set(numbers)
        .at[student_places]
        .set(numbers)[:dump]
    )
    padded = jnp.concatenate([tokens, jnp.zeros((1, width), jnp.bfloat16)], axis=0)
    outgoing = padded[owners].reshape(experts, capacity, width)
    weight_in = expert_in[0]
    weight_out = expert_out[0]
    narrow = width // shards
    section = lax.dynamic_slice_in_dim(outgoing, lax.axis_index(VOCAB) * narrow, narrow, 2)
    hidden = jax.nn.gelu(
        jnp.einsum(
            "nkd,df->nkf",
            gather_axes(
                lax.all_to_all(section, "expert", split_axis=0, concat_axis=0, tiled=True),
                ("vocab_0", "vocab_1"),
                2,
            ),
            weight_in,
            preferred_element_type=jnp.float32,
        )
    ).astype(jnp.bfloat16)
    unsummed = jnp.einsum("nkf,fd->nkd", hidden, weight_out, preferred_element_type=jnp.float32)
    shares = sum_in_two_steps(unsummed, ("vocab_0", "vocab_1"), 2)
    returned = lax.all_to_all(
        shares.astype(jnp.bfloat16), "expert", split_axis=0, concat_axis=0, tiled=True
    )
    flattened = returned.reshape(dump, returned.shape[2])
    flattened = jnp.concatenate(
        [flattened, jnp.zeros((1, flattened.shape[1]), jnp.bfloat16)], axis=0
    )
    teacher_part = flattened[teacher_places]
    student_part = flattened[student_places]
    teacher_branch, student_branch = side_by_side(
        (teacher_part, student_part), ("vocab_0", "vocab_1"), 1, 0
    )
    teacher_normed = normed(tokens, teacher_branch, teacher_gain)
    student_normed = normed(tokens, student_branch, student_gain)
    lowest = jnp.full((count,), -1e30, jnp.float32)
    pieces = sent_together((teacher_head, student_head), "expert", 0, 1)
    teacher_peak = lowest
    student_peak = lowest
    teacher_logits = lax.dot_general(
        teacher_normed, pieces[0], (((1,), (1,)), ((), ())), preferred_element_type=jnp.float32
    )
    student_logits = lax.dot_general(
        student_normed, pieces[1], (((1,), (1,)), ((), ())), preferred_element_type=jnp.float32
    )
    new_teacher = jnp.maximum(teacher_peak, jnp.max(teacher_logits, axis=1))
    new_student = jnp.maximum(student_peak, jnp.max(student_logits, axis=1))
    teacher_exps = jnp.exp(teacher_logits - new_teacher[:, None])
    teacher_total = jnp.sum(teacher_exps, axis=1)
    weighted = jnp.sum(teacher_exps * (teacher_logits - student_logits), axis=1)
    student_total = jnp.sum(jnp.exp(student_logits - new_student[:, None]), axis=1)
    local_stats = (new_teacher, teacher_total, new_student, student_total, weighted)
    teacher_peak, teacher_total, student_peak, student_total, weighted = combined_all(
        local_stats, VOCAB, combine_stats
    )
    return (
        weighted / teacher_total
        - teacher_peak
        - jnp.log(teacher_total)
        + student_peak
        + jnp.log(student_total)
    )


def solution(mesh):
    split = Mesh(mesh.devices.reshape(mesh.shape["expert"], 4, 2), ("expert", "vocab_0", "vocab_1"))
    placed = (
        P("expert", None),
        P("expert", None),
        P("expert", None),
        P("expert", None),
        P("expert", None, VOCAB),
        P("expert", VOCAB, None),
        P(),
        P(),
        P(VOCAB_EXPERT, None),
        P(VOCAB_EXPERT, None),
    )
    return jax.shard_map(local, mesh=split, in_specs=placed, out_specs=P("expert"), check_vma=False)
```

profile of v0, /device:TPU:1, one launch (start us, length us, event | category | flops | bytes accessed | tf_op | source)
XLA Modules:
  0.0 239.8 jit_solution(9598050706206735160)
XLA Ops:
  6.6 2.0 pad_maximum_fusion
  8.6 0.1 concatenate.15
  8.7 0.3 convert_reduce_fusion
  9.0 1.4 scatter_custom_fusion
  10.5 1.4 scatter_fusion
  11.9 4.3 %gather_fusion = bf16[768,2048]{1,0:T(8,128)(2,1)} fusion(bf16[257,2048]{1,0:T(8,128)(2,1)S(1)} %concatenate.15, s32[1024]{0:T(1024)S(1)} %pad_clamp_fusion.2), kind=kCustom, calls=%fused_computation | custom fusion | bytes 6294528 | tf_op jit(solution)/shard_map/gather | solution.py:156
  16.2 1.0 constant_dynamic-slice_fusion
  17.2 30.0 %all_to_all.45 = bf16[32,24,256]{2,1,0:T(8,128)(2,1)S(1)} all-to-all(bf16[32,24,256]{2,1,0:T(8,128)(2,1)S(1)} %constant_dynamic-slice_fusion), channel_id=1, replica_groups=mesh['expert'=32,'vocab_0'=4,'vocab_1'=2] {'expert'}, dimensions={0} | all-to-all | bytes 786432 | tf_op jit(solution)/shard_map/all_to_all | solution.py:165
  47.3 1.3 broadcast_in_dim.24
  48.5 4.0 %all-to-all-start.1 = ((bf16[4,32,24,256]{3,2,1,0:T(8,128)(2,1)}), bf16[4,32,24,256]{3,2,1,0:T(8,128)(2,1)S(1)}, u32[]{:S(2)}, u32[]{:S(2)}) async-start(bf16[4,32,24,256]{3,2,1,0:T(8,128)(2,1)} %broadcast_in_dim.24), calls=%async_computation.1 | async-start | bytes 3145728 | tf_op jit(solution)/shard_map/all_to_all | solution.py:33
  52.6 6.4 %copy.85 = bf16[2048,1024]{1,0:T(8,128)(2,1)} copy(bf16[2048,1024]{0,1:T(8,128)(2,1)} %bitcast.87) | data formatting | bytes 8388608 | tf_op jit(solution)/shard_map/nkf,fd->nkd/dot_general | solution.py:173
  59.0 11.6 %all-to-all-done.1 = bf16[4,32,24,256]{3,2,1,0:T(8,128)(2,1)S(1)} async-done(((bf16[4,32,24,256]{3,2,1,0:T(8,128)(2,1)}), bf16[4,32,24,256]{3,2,1,0:T(8,128)(2,1)S(1)}, u32[]{:S(2)}, u32[]{:S(2)}) %all-to-all-start.1) | async-done | bytes 1572896 | tf_op jit(solution)/shard_map/all_to_all | solution.py:33
  70.6 1.2 copy.69
  71.8 1.5 broadcast_in_dim.25
  73.3 9.6 %all_to_all.46 = bf16[2,4,32,24,256]{4,1,3,2,0:T(4,128)(2,1)S(1)} all-to-all(bf16[2,4,32,24,256]{4,1,3,2,0:T(4,128)(2,1)S(1)} %broadcast_in_dim.25), channel_id=1, replica_groups=mesh['expert'=32,'vocab_0'=4,'vocab_1'=2] {'vocab_1'}, dimensions={0} | all-to-all | bytes 6291456 | tf_op jit(solution)/shard_map/all_to_all | solution.py:33
  83.0 0.4 copy.70
  83.4 0.4 copy.93
  83.8 1.9 copy-done.10
  85.7 4.0 %fusion.13 = bf16[32,24,1024]{2,1,0:T(8,128)(2,1)S(1)} fusion(bf16[32,24,2048]{2,1,0:T(8,128)(2,1)S(1)} %bitcast.90, bf16[1,2048,1024]{2,1,0:T(8,128)(2,1)S(1)} %copy-done.10), kind=kOutput, calls=%fused_computation.20 | convolution fusion | flops 3228303360 | bytes 8912896 | tf_op jit(solution)/shard_map/nkd,df->nkf/dot_general | solution.py:162
  89.7 3.5 %fusion.17 = f32[32,24,4,512]{3,1,2,0:T(8,128)S(1)} fusion(bf16[4,512,1024,1]{2,1,0,3:T(8,128)(2,1)S(1)} %bitcast.88, bf16[32,24,1024]{2,1,0:T(8,128)(2,1)S(1)} %fusion.13), kind=kOutput, calls=%fused_computation.31 | convolution fusion | flops 3221225472 | bytes 12058624 | tf_op jit(solution)/shard_map/nkf,fd->nkd/dot_general | solution.py:173
  93.2 0.9 copy.100
  94.1 10.0 %all_to_all.47 = f32[2,4,32,24,256]{4,3,1,2,0:T(8,128)} all-to-all(f32[2,4,32,24,256]{4,3,1,2,0:T(8,128)S(1)} %bitcast.83), channel_id=1, replica_groups=mesh['expert'=32,'vocab_0'=4,'vocab_1'=2] {'vocab_1'}, dimensions={0} | all-to-all | bytes 12582912 | tf_op jit(solution)/shard_map/all_to_all | solution.py:19
  104.1 3.8 %reduce_sum.89 = f32[4,32,24,256]{3,2,0,1:T(8,128)S(1)} reduce(f32[2,4,32,24,256]{4,3,1,2,0:T(8,128)} %all_to_all.47, f32[]{:T(128)} %constant.18.clone.1), dimensions={0}, to_apply=%region_4.5 | reduce | flops 786432 | bytes 9437188 | tf_op jit(solution)/shard_map/reduce_sum | solution.py:20
  107.9 0.3 copy.75
  108.2 39.9 %all_to_all.48 = f32[4,32,24,256]{3,2,1,0:T(8,128)S(1)} all-to-all(f32[4,32,24,256]{3,2,1,0:T(8,128)S(1)} %copy.75), channel_id=1, replica_groups=mesh['expert'=32,'vocab_0'=4,'vocab_1'=2] {'vocab_0'}, dimensions={0} | all-to-all | bytes 6291456 | tf_op jit(solution)/shard_map/all_to_all | solution.py:27
  148.1 1.0 reduce_sum.90
  149.1 4.6 %all-to-all-start.5 = ((bf16[32,24,256]{2,1,0:T(8,128)(2,1)}), bf16[32,24,256]{2,1,0:T(8,128)(2,1)S(1)}, u32[]{:S(2)}, u32[]{:S(2)}) async-start(bf16[32,24,256]{2,1,0:T(8,128)(2,1)} %reduce_sum.90), calls=%async_computation.5 | async-start | bytes 786432 | tf_op jit(solution)/shard_map/all_to_all | solution.py:175
  153.7 15.4 %all-to-all-done.5 = bf16[32,24,256]{2,1,0:T(8,128)(2,1)S(1)} async-done(((bf16[32,24,256]{2,1,0:T(8,128)(2,1)}), bf16[32,24,256]{2,1,0:T(8,128)(2,1)S(1)}, u32[]{:S(2)}, u32[]{:S(2)}) %all-to-all-start.5) | async-done | bytes 393248 | tf_op jit(solution)/shard_map/all_to_all | solution.py:175
  169.2 1.2 gather_fusion.2
  170.4 1.2 gather_fusion.1
  171.6 1.1 broadcast_in_dim.26
  172.6 3.8 %all-to-all-start.6 = ((bf16[4,512,256]{2,1,0:T(8,128)(2,1)}), bf16[4,512,256]{2,1,0:T(8,128)(2,1)S(1)}, u32[]{:S(2)}, u32[]{:S(2)}) async-start(bf16[4,512,256]{2,1,0:T(8,128)(2,1)} %broadcast_in_dim.26), calls=%async_computation.6 | async-start | bytes 2097152 | tf_op jit(solution)/shard_map/all_to_all | solution.py:33
  176.4 0.5 copy.68
  177.0 12.6 %all-to-all-done.6 = bf16[4,512,256]{2,1,0:T(8,128)(2,1)S(1)} async-done(((bf16[4,512,256]{2,1,0:T(8,128)(2,1)}), bf16[4,512,256]{2,1,0:T(8,128)(2,1)S(1)}, u32[]{:S(2)}, u32[]{:S(2)}) %all-to-all-start.6) | async-done | bytes 1048608 | tf_op jit(solution)/shard_map/all_to_all | solution.py:33
  189.5 0.8 copy.76
  190.3 0.5 broadcast_in_dim.27
  190.9 8.0 %all_to_all.49 = bf16[2,4,512,256]{3,1,2,0:T(4,128)(2,1)S(1)} all-to-all(bf16[2,4,512,256]{3,1,2,0:T(4,128)(2,1)S(1)} %broadcast_in_dim.27), channel_id=1, replica_groups=mesh['expert'=32,'vocab_0'=4,'vocab_1'=2] {'vocab_1'}, dimensions={0} | all-to-all | bytes 4194304 | tf_op jit(solution)/shard_map/all_to_all | solution.py:33
  198.9 0.3 copy.77
  199.2 2.4 %slice_convert_fusion = (f32[256,8,256]{2,0,1:T(8,128)}, f32[256,8,256]{2,0,1:T(8,128)}) fusion(bf16[512,8,256]{2,0,1:T(8,128)(2,1)S(1)} %bitcast.85), kind=kLoop, calls=%fused_computation.33 | loop fusion | flops 1048576 | bytes 6291456 | tf_op jit(solution)/shard_map/convert_element_type | solution.py:106
  201.6 1.9 copy.79
  203.5 2.9 %copy.78 = f32[256,8,256]{0,2,1:T(8,128)} copy(f32[256,8,256]{2,0,1:T(8,128)} %get-tuple-element.21) | data formatting | bytes 4194304 | tf_op jit(solution)/shard_map/convert_element_type | solution.py:106
  206.4 2.5 %multiply_reduce_fusion.1 = (f32[256]{0:T(256)S(1)}, f32[256]{0:T(256)S(1)}) fusion(f32[256,8,256]{0,2,1:T(8,128)S(1)} %copy.79, bf16[256,2048]{0,1:T(8,128)(2,1)S(1)} %copy.68, f32[256,8,256]{0,2,1:T(8,128)} %copy.78), kind=kLoop, calls=%fused_computation.26 | loop fusion | flops 3669504 | bytes 5244928 | tf_op jit(solution)/shard_map/reduce_sum | solution.py:107
  208.9 2.0 multiply_convert_fusion
  210.9 6.3 %fusion.26 = (f32[256]{0:T(256)S(1)}, f32[256,2048]{1,0:T(8,128)S(1)}) fusion(bf16[256,2048]{0,1:T(8,128)(2,1)} %get-tuple-element.23, bf16[2048,4096]{1,0:T(8,128)(2,1)} %all-gather.2.cloned.1.call-done), kind=kOutput, calls=%fused_computation.86 | convolution fusion | flops 2148007680 | bytes 11535360 | tf_op jit(solution)/shard_map/dot_general | solution.py:193
  217.2 5.9 %fusion.27 = (f32[256]{0:T(256)S(1)}, f32[256,2048]{1,0:T(8,128)S(1)}) fusion(bf16[256,2048]{0,1:T(8,128)(2,1)S(1)} %copy-done.4, bf16[2048,4096]{1,0:T(8,128)(2,1)} %all-gather.2.cloned.1.call-done), kind=kOutput, calls=%fused_computation.87 | convolution fusion | flops 2148007680 | bytes 11535360 | tf_op jit(solution)/shard_map/dot_general | solution.py:196
  223.1 1.0 multiply_reduce_fusion
  224.1 7.6 %all_to_all.50 = f32[8,5,256]{2,1,0:T(8,128)S(1)} all-to-all(f32[8,5,256]{2,1,0:T(8,128)S(1)} %broadcast_in_dim.29), channel_id=1, replica_groups=mesh['expert'=32,'vocab_0'=4,'vocab_1'=2] {'vocab_0','vocab_1'}, dimensions={0} | all-to-all | bytes 81920 | tf_op jit(solution)/shard_map/all_to_all | solution.py:33
  232.3 0.6 log_add_fusion
  (71 shorter events, 0.8 us)
Async XLA Ops:
  6.5 2.0 copy-start.1
  6.5 2.2 copy-start.6
  6.5 2.2 copy-start.9
  6.5 2.2 copy-start.5
  6.5 204.4 %all-gather.2.cloned.1.call-start = ((), (), s32[]{:S(2)}) async-start(), calls=%async_computation.9 | async-start | bytes 17301504 | tf_op jit(solution)/shard_map/all_gather | solution.py:64
  48.5 22.0 %all-to-all-start.1 = ((bf16[4,32,24,256]{3,2,1,0:T(8,128)(2,1)}), bf16[4,32,24,256]{3,2,1,0:T(8,128)(2,1)S(1)}, u32[]{:S(2)}, u32[]{:S(2)}) async-start(bf16[4,32,24,256]{3,2,1,0:T(8,128)(2,1)} %broadcast_in_dim.24), calls=%async_computation.1 | async-start | bytes 3145728 | tf_op jit(solution)/shard_map/all_to_all | solution.py:33
  83.4 2.3 copy-start.10
  85.7 4.0 %copy-start.3 = (bf16[2048,1024]{1,0:T(8,128)(2,1)S(1)}, bf16[2048,1024]{1,0:T(8,128)(2,1)}, u32[]{:S(2)}) copy-start(bf16[2048,1024]{1,0:T(8,128)(2,1)} %copy.85) | copy-start | bytes 12582916
  149.1 20.1 %all-to-all-start.5 = ((bf16[32,24,256]{2,1,0:T(8,128)(2,1)}), bf16[32,24,256]{2,1,0:T(8,128)(2,1)S(1)}, u32[]{:S(2)}, u32[]{:S(2)}) async-start(bf16[32,24,256]{2,1,0:T(8,128)(2,1)} %reduce_sum.90), calls=%async_computation.5 | async-start | bytes 786432 | tf_op jit(solution)/shard_map/all_to_all | solution.py:175
  171.5 4.9 %copy-start.2 = (bf16[256,2048]{1,0:T(8,128)(2,1)S(1)}, bf16[256,2048]{1,0:T(8,128)(2,1)}, u32[]{:S(2)}) copy-start(bf16[256,2048]{1,0:T(8,128)(2,1)} %param.10) | copy-start | bytes 3145732
  172.6 16.9 %all-to-all-start.6 = ((bf16[4,512,256]{2,1,0:T(8,128)(2,1)}), bf16[4,512,256]{2,1,0:T(8,128)(2,1)S(1)}, u32[]{:S(2)}, u32[]{:S(2)}) async-start(bf16[4,512,256]{2,1,0:T(8,128)(2,1)} %broadcast_in_dim.26), calls=%async_computation.6 | async-start | bytes 2097152 | tf_op jit(solution)/shard_map/all_to_all | solution.py:33
  206.4 2.5 %copy-start = (f32[256,8,256]{0,2,1:T(8,128)S(1)}, f32[256,8,256]{0,2,1:T(8,128)}, u32[]{:S(2)}) copy-start(f32[256,8,256]{0,2,1:T(8,128)} %copy.78) | copy-start | bytes 6291460
  206.4 2.5 %copy-start.7 = (f32[2048]{0:T(1024)S(1)}, f32[2048]{0:T(1024)}, u32[]{:S(2)}) copy-start(f32[2048]{0:T(1024)} %param.17) | copy-start | bytes 24580
  206.4 2.5 %copy-start.8 = (f32[2048]{0:T(1024)S(1)}, f32[2048]{0:T(1024)}, u32[]{:S(2)}) copy-start(f32[2048]{0:T(1024)} %param.16) | copy-start | bytes 24580
  210.9 6.3 %copy-start.4 = (bf16[256,2048]{0,1:T(8,128)(2,1)S(1)}, bf16[256,2048]{0,1:T(8,128)(2,1)}, u32[]{:S(2)}) copy-start(bf16[256,2048]{0,1:T(8,128)(2,1)} %get-tuple-element.22) | copy-start | bytes 3145732
Sparse Core Ops, SparseCore 0:
  9.9 150.0 all-gather.1
where the time goes:
time: 241 us; the launch traced here: 240 us
  blocking collectives  105 us (44%)
  waiting for transfers between devices  39.6 us (16%)
  local copies, waits for them, and re-layouts  33.5 us (14%)
  matrix products  19.6 us (8%)
  other arithmetic  15.7 us (7%)
  between operations  13.8 us (6%)
  starting transfers between devices  12.4 us (5%)
    all_to_all x1, blocking collectives, sum_in_two_steps(): lax.all_to_all(nearer, far, split_axis=0, concat_axis=0, tiled=True)  39.9 us
    all_to_all x1, blocking collectives, local(): lax.all_to_all(section, 'expert', split_axis=0, concat_axis=0, tiled=True)  30 us
    all_to_all x3, blocking collectives, copy_for_each(): lax.all_to_all(jnp.broadcast_to(array[None], (count, *array.shape)), axis...  25.2 us
    all_to_all x2, waiting for transfers between devices, copy_for_each(): lax.all_to_all(jnp.broadcast_to(array[None], (count, *array.shape)), axis...  24.2 us
    all_to_all x1, waiting for transfers between devices, local(): lax.all_to_all(shares.astype(jnp.bfloat16), 'expert', split_axis=0, conca...  15.4 us
    all_to_all x1, blocking collectives, sum_at_owner(): lax.all_to_all(blocks, axis, split_axis=0, concat_axis=0, tiled=True)  9.95 us
    all_to_all x2, starting transfers between devices, copy_for_each(): lax.all_to_all(jnp.broadcast_to(array[None], (count, *array.shape)), axis...  7.84 us
    dot_general x1, local copies, waits for them, and re-layouts, local(): jnp.einsum('nkf,fd->nkd', hidden, weight_out, preferred_element_type=jnp....  6.41 us
  transfers between devices with their start and end apart: 4, of which 3 were waited for; matrix products, arithmetic and copies ran while one was open for 21% of the time, Pallas kernels for 0%

commit v1 on v0

v1 whole, which is shorter than its diff:
```python
import jax
import jax.numpy as jnp
from jax import lax
from jax.experimental import pallas as pl
from jax.experimental.pallas import tpu as pltpu
from jax.sharding import PartitionSpec as P

MESH = pl.DeviceIdType.MESH
BF = jnp.bfloat16
F32 = jnp.float32
CAP = 24
NT = (((1,), (1,)), ((), ()))


def gelu(v):
    return 0.5 * v * (1.0 + jnp.tanh(0.7978845608028654 * (v + 0.044715 * v * v * v)))


def kernel(
    tok_hbm, te_ref, se_ref, pr_ref, win_hbm, wout_hbm, tg_ref, sg_ref, th_hbm, sh_hbm,
    o_ref,
    tok, out_rows, feats, w1, w2, acc, hid, part_send, part_recv, own_part,
    back, ret, unit, units, heads, st_send, st_recv, pick,
    load_sem, w_send, w_recv, disp_send, disp_recv, xag_send, xag_recv,
    rs_send, rs_recv, comb_send, comb_recv, pair_send, pair_recv,
    ag_send, ag_recv, hd_send, hd_recv, hp_send, hp_recv, st_ssem, st_rsem,
):
    e = lax.axis_index("expert")
    v = lax.axis_index("vocab")
    z, y = e // 4, e % 4
    x, c = v // 2, v % 2
    mate = 1 - c
    home = e // 16

    def at(zz, yy, xx, cc):
        return (zz * 4 + yy, xx * 2 + cc)

    def step(a, d, n):
        return lax.rem(a + d + n, n)

    xr, xl, xo = step(x, 1, 4), step(x, -1, 4), step(x, 2, 4)

    def remote(src, dst, ssem, rsem, dev):
        return pltpu.make_async_remote_copy(
            src_ref=src, dst_ref=dst, send_sem=ssem, recv_sem=rsem,
            device_id=dev, device_id_type=MESH,
        )

    cp_tok = pltpu.make_async_copy(
        tok_hbm.at[:, pl.ds(pl.multiple_of(v * 256, 256), 256)], tok, load_sem.at[0]
    )
    cp_tok.start()
    cp_w1 = pltpu.make_async_copy(win_hbm.at[0], w1.at[c], load_sem.at[1])
    cp_w2 = pltpu.make_async_copy(wout_hbm.at[0], w2.at[c], load_sem.at[2])
    cp_th = pltpu.make_async_copy(th_hbm, heads.at[z, c, 0], load_sem.at[3])
    cp_sh = pltpu.make_async_copy(sh_hbm, heads.at[z, c, 1], load_sem.at[4])
    rw1 = remote(win_hbm.at[0], w1.at[c], w_send.at[0], w_recv.at[0], at(z, y, x, mate))
    rw2 = remote(wout_hbm.at[0], w2.at[c], w_send.at[1], w_recv.at[1], at(z, y, x, mate))
    rw1.start()
    cp_w1.start()

    def spread(row):
        return jnp.broadcast_to(row.astype(F32), (256, 256))

    pj = spread(pr_ref[...])
    pi = pj.T

    def places(expert_ref, lane):
        ej = spread(expert_ref[...])
        ei = ej.T
        same = ei == ej
        rank_row = jnp.sum(jnp.where(same & (pi < pj), 1.0, 0.0), axis=0, keepdims=True)
        rank_col = jnp.sum(jnp.where(same & (pj < pi), 1.0, 0.0), axis=1, keepdims=True)

        def place(expert, rank):
            return jnp.where(rank < CAP, (2.0 * expert + lane) * CAP + rank, -1.0)

        return place(ej[:1], rank_row), place(ei[:, :1], rank_col)

    t_row, t_col = places(te_ref, 0.0)
    s_row, s_col = places(se_ref, 1.0)
    slot = lax.broadcasted_iota(jnp.int32, (768, 256), 0).astype(F32)
    gather = jnp.where((slot == t_row) | (slot == s_row), 1.0, 0.0).astype(BF)
    lanes = lax.broadcasted_iota(jnp.int32, (256, 768), 1).astype(F32)
    pick[0:256] = jnp.where(lanes == t_col, 1.0, 0.0).astype(BF)
    pick[256:512] = jnp.where(lanes == s_col, 1.0, 0.0).astype(BF)
    cp_tok.wait()
    picked = jnp.dot(gather, tok[...], preferred_element_type=F32)
    out_rows[...] = picked.reshape(96, 8, 256).astype(BF)

    my_slot = pl.ds(3 * lax.rem(e, 16), 3)

    def disp(to):
        return remote(
            out_rows.at[pl.ds(3 * to, 3)], feats.at[x, c, my_slot],
            disp_send.at[to], disp_recv.at[lax.rem(e, 16), c], (to, x * 2 + home),
        )

    cp_self = pltpu.make_async_copy(
        out_rows.at[pl.ds(3 * e, 3)], feats.at[x, c, my_slot], load_sem.at[5]
    )

    @pl.when(home == c)
    def _():
        cp_self.start()

    @pl.when(home != c)
    def _():
        disp(e).start()

    def send_rows(r, carry):
        disp(lax.rem(e + r, 32)).start()
        return carry

    lax.fori_loop(1, 32, send_rows, 0)
    rw2.start()
    cp_w2.start()
    cp_th.start()
    cp_sh.start()

    def arrived_rows(cc, j):
        here = feats.at[x, cc, pl.ds(3 * j, 3)]
        return remote(
            here, here, disp_send.at[0], disp_recv.at[j, cc], at(z, y, x, mate)
        )

    def wait_rows(cc):
        def wait_one(j, carry):
            @pl.when(jnp.logical_not((c * 16 + j == e) & (cc == c)))
            def _():
                arrived_rows(cc, j).wait_recv()

            return carry

        lax.fori_loop(0, 16, wait_one, 0)

    @pl.when(home == c)
    def _():
        cp_self.wait()

    def xcopy(xx, cc, k, to):
        piece = feats.at[xx, cc]
        return remote(piece, piece, xag_send.at[k], xag_recv.at[k], at(z, y, to, c))

    wait_rows(0)
    xcopy(x, 0, 0, xr).start()
    wait_rows(1)
    xcopy(x, 1, 1, xl).start()
    xcopy(x, 1, 2, xr).start()
    xcopy(x, 0, 3, xl).start()

    zu, zd = step(z, 1, 8), step(z, -1, 8)
    cp_th.wait()
    cp_sh.wait()

    def ring_up(zz, k, both):
        piece = heads.at[zz, c] if both else heads.at[zz, c, 0]
        return remote(piece, piece, hd_send.at[0, k], hd_recv.at[0, k], at(zu, y, x, c))

    def ring_down(zz, k, both):
        piece = heads.at[zz, c] if both else heads.at[zz, c, 1]
        return remote(piece, piece, hd_send.at[1, k], hd_recv.at[1, k], at(zd, y, x, c))

    def to_mate(zz, cc, k):
        piece = heads.at[zz, cc]
        return remote(piece, piece, hp_send.at[k], hp_recv.at[k], at(z, y, x, mate))

    ring_up(z, 0, True).start()
    ring_down(z, 0, True).start()
    to_mate(z, c, 0).start()

    cp_w1.wait()
    rw1.wait_recv()

    def rows_of(xx):
        return [
            feats[xx, cc].astype(F32).reshape(384, 256).astype(BF) for cc in (0, 1)
        ]

    def hidden_pass(xs, first, last):
        for cc in (0, 1):
            def body(n, carry):
                cols = pl.ds(pl.multiple_of(n * 256, 256), 256)
                total = None if first else acc[cc, :, cols]
                for xx in xs:
                    left = jnp.concatenate(rows_of(xx), axis=1)
                    k = pl.ds(pl.multiple_of(xx * 512, 512), 512)
                    term = jnp.dot(left, w1[cc, k, cols], preferred_element_type=F32)
                    total = term if total is None else total + term
                if last:
                    hid[cc, :, cols] = gelu(total).astype(BF)
                else:
                    acc[cc, :, cols] = total
                return carry

            lax.fori_loop(0, 4, body, 0)

    hidden_pass([x], True, False)
    xcopy(xl, 0, 0, xr).wait_recv()
    xcopy(xl, 0, 4, xr).start()
    xcopy(xr, 1, 1, xl).wait_recv()
    xcopy(xr, 1, 5, xl).start()
    xcopy(xl, 1, 2, xr).wait_recv()
    xcopy(xr, 0, 3, xl).wait_recv()
    hidden_pass([xl, xr], False, False)
    xcopy(xo, 0, 4, xr).wait_recv()
    xcopy(xo, 1, 5, xl).wait_recv()

    def ring_next(k):
        lo, hi = step(z, -k, 8), step(z, k, 8)
        ring_up(lo, k - 1, True).wait_recv()
        ring_down(hi, k - 1, True).wait_recv()
        ring_up(lo, k, k < 3).start()
        ring_down(hi, k, k < 3).start()
        to_mate(lo, c, 2 * k - 1).start()
        to_mate(hi, c, 2 * k).start()

    ring_next(1)
    hidden_pass([xo], False, True)

    cp_w2.wait()
    rw2.wait_recv()

    def partial(xx, half):
        cols = pl.ds(pl.multiple_of(xx * 512 + half * 256, 256), 256)
        return jnp.dot(hid[0], w2[0, :, cols], preferred_element_type=F32) + jnp.dot(
            hid[1], w2[1, :, cols], preferred_element_type=F32
        )

    def rs(k, to):
        return remote(
            part_send.at[k], part_recv.at[k], rs_send.at[k], rs_recv.at[k], at(z, y, to, c)
        )

    part_send[0] = partial(xo, 0).astype(BF)
    rs(0, xr).start()
    part_send[1] = partial(xo, 1).astype(BF)
    rs(1, xl).start()
    part_send[2] = partial(xr, 1).astype(BF)
    rs(2, xr).start()
    part_send[3] = partial(xl, 0).astype(BF)
    rs(3, xl).start()
    mine = partial(xr, 0)
    rs(0, xr).wait_recv()
    part_send[4] = (mine + part_recv[0].astype(F32)).astype(BF)
    rs(4, xr).start()
    mine = partial(xl, 1)
    rs(1, xl).wait_recv()
    part_send[5] = (mine + part_recv[1].astype(F32)).astype(BF)
    rs(5, xl).start()
    own_part[0] = partial(x, 0)
    own_part[1] = partial(x, 1)
    ring_next(2)
    rs(2, xr).wait_recv()
    rs(3, xl).wait_recv()

    def comb(b, cc):
        return remote(
            back.at[cc, pl.ds(3 * lax.rem(b, 16), 3)], ret.at[pl.ds(3 * e, 3)],
            comb_send.at[cc, lax.rem(b, 16)], comb_recv.at[e], (b, x * 2 + cc),
        )

    def send_back(cc):
        def one(r, carry):
            b = c * 16 + lax.rem(e + r, 16)

            @pl.when(jnp.logical_not((b == e) & (cc == c)))
            def _():
                comb(b, cc).start()

            return carry

        lax.fori_loop(0, 16, one, 0)

    rs(4, xr).wait_recv()
    total = own_part[0] + part_recv[3].astype(F32) + part_recv[4].astype(F32)
    back[0] = total.reshape(48, 8, 256).astype(BF)
    send_back(0)
    rs(5, xl).wait_recv()
    total = own_part[1] + part_recv[2].astype(F32) + part_recv[5].astype(F32)
    back[1] = total.reshape(48, 8, 256).astype(BF)
    send_back(1)
    cp_back = pltpu.make_async_copy(
        back.at[c, pl.ds(3 * lax.rem(e, 16), 3)], ret.at[pl.ds(3 * e, 3)], load_sem.at[6]
    )

    @pl.when(home == c)
    def _():
        cp_back.start()
        cp_back.wait()

    def wait_back(r, carry):
        @pl.when(jnp.logical_not((r == e) & (home == c)))
        def _():
            here = ret.at[pl.ds(3 * r, 3)]
            remote(
                here, here, comb_send.at[0, 0], comb_recv.at[r], at(z, y, x, mate)
            ).wait_recv()

        return carry

    lax.fori_loop(0, 32, wait_back, 0)
    ring_next(3)

    rows = ret[...].astype(F32).reshape(768, 256).astype(BF)
    stream = tok[...].astype(F32)
    squares = []
    cols = pl.ds(pl.multiple_of(v * 256, 256), 256)
    for k, gain_ref in enumerate((tg_ref, sg_ref)):
        branch = jnp.dot(
            pick[256 * k : 256 * k + 256], rows, preferred_element_type=F32
        )
        summed = stream + branch
        scaled = (summed * gain_ref[:, cols]).astype(BF)
        unit[0, 128 * k : 128 * k + 128] = scaled[:128]
        unit[1, 128 * k : 128 * k + 128] = scaled[128:]
        column = jnp.sum(summed * summed, axis=1, keepdims=True)
        squares.append(jnp.broadcast_to(column, (256, 128)).T[:1])
    low = lax.broadcasted_iota(jnp.int32, (16, 256), 0) == 0
    for h in (0, 1):
        lines = []
        for k in (0, 1):
            part = squares[k][:, 128 * h : 128 * h + 128]
            top = part.astype(BF).astype(F32)
            lines.append(
                jnp.broadcast_to(jnp.concatenate([top, part - top], axis=1), (16, 256))
            )
        unit[h, 256:272] = jnp.where(low, lines[0], lines[1]).astype(BF)
    swap = remote(
        unit.at[mate], units.at[y, x, c], pair_send.at[0], pair_recv.at[0], at(z, y, x, mate)
    )
    swap.start()
    cp_unit = pltpu.make_async_copy(unit.at[c], units.at[y, x, c], load_sem.at[7])
    cp_unit.start()
    cp_unit.wait()
    remote(
        unit.at[mate], units.at[y, x, mate], pair_send.at[0], pair_recv.at[0],
        at(z, y, x, mate),
    ).wait_recv()

    here = (x, y)

    def place_of(axis, a, b):
        return units.at[b, a, 0] if axis == 0 else units.at[a, b, 1]

    def dev_of(axis, d):
        p, q = (step(x, d, 4), y) if axis == 0 else (x, step(y, d, 4))
        return at(z, q, p, c)

    def hop(axis, along, a, b, k, d, rows_=None):
        piece = place_of(axis, a, b)
        if rows_ is not None:
            piece = piece.at[rows_[0] : rows_[1]]
        return remote(piece, piece, ag_send.at[axis, k], ag_recv.at[axis, k], dev_of(along, d))

    halves = ((0, 128), (128, 272))

    def first(axis, k, off, d, rows_=None):
        a = step(here[axis], off, 4)
        return hop(axis, axis, a, here[1 - axis], k, d, rows_)

    def second(axis, rel, off, kind, d):
        a = step(here[axis], rel, 4)
        b = step(here[1 - axis], off, 4)
        return hop(axis, 1 - axis, a, b, 4 + 3 * rel + kind, d)

    both = (0, 1)
    for axis in both:
        first(axis, 0, 0, 1).start()
        first(axis, 1, 0, -1).start()
    for axis in both:
        second(axis, 0, 0, 0, 1).start()
        second(axis, 0, 0, 1, -1).start()
    for axis in both:
        first(axis, 0, -1, 1).wait_recv()
        first(axis, 2, -1, 1, halves[0]).start()
        first(axis, 1, 1, -1).wait_recv()
        first(axis, 3, 1, -1, halves[1]).start()
    for axis in both:
        for rel in (3, 1):
            second(axis, rel, 0, 0, 1).start()
            second(axis, rel, 0, 1, -1).start()
    for axis in both:
        first(axis, 2, 2, 1, halves[0]).wait_recv()
        first(axis, 3, 2, -1, halves[1]).wait_recv()
        second(axis, 2, 0, 0, 1).start()
        second(axis, 2, 0, 1, -1).start()
    for rel in (0, 3, 1, 2):
        for axis in both:
            second(axis, rel, -1, 0, 1).wait_recv()
            second(axis, rel, 1, 1, -1).wait_recv()
            if rel in (0, 1):
                second(axis, rel, -1, 2, 1).start()
            else:
                second(axis, rel, 1, 2, -1).start()
    ring_up(step(z, 4, 8), 3, False).wait_recv()
    ring_down(step(z, 4, 8), 3, False).wait_recv()
    to_mate(step(z, 4, 8), c, 7).start()
    for k in range(8):
        off = 0 if k == 0 else (4 if k == 7 else ((k + 1) // 2) * (-1 if k % 2 else 1))
        to_mate(step(z, off, 8), mate, k).wait_recv()
    for rel in (0, 3, 1, 2):
        for axis in both:
            second(axis, rel, 2, 2, 1 if rel in (0, 1) else -1).wait_recv()

    for pair in (0, 1):
        scales = []
        for k in (0, 1):
            parts = []
            for yy in (2 * pair, 2 * pair + 1):
                total = jnp.zeros((1, 128), F32)
                for xx in range(4):
                    for cc in (0, 1):
                        line = units[yy, xx, cc, 256:272, :].astype(F32)[k : k + 1]
                        total = total + line[:, :128] + line[:, 128:]
                parts.append(lax.rsqrt(total * (1.0 / 2048.0) + 1e-5))
            scales.append(jnp.concatenate(parts, axis=1))

        def logits(k, zz):
            left = heads[pl.ds(zz, 4), :, k].reshape(512, 2048)
            total = None
            for xx in range(4):
                for cc in (0, 1):
                    right = jnp.concatenate(
                        [
                            units[2 * pair + i, xx, cc, 128 * k : 128 * k + 128, :]
                            for i in (0, 1)
                        ],
                        axis=0,
                    )
                    kk = (xx * 2 + cc) * 256
                    term = lax.dot_general(
                        left[:, kk : kk + 256], right, NT, preferred_element_type=F32
                    )
                    total = term if total is None else total + term
            return total * scales[k]

        def chunk(n, carry):
            tm, ts, tw, sm, ss = carry
            tl = logits(0, 4 * n)
            sl = logits(1, 4 * n)
            tm2 = jnp.maximum(tm, jnp.max(tl, axis=0, keepdims=True))
            sm2 = jnp.maximum(sm, jnp.max(sl, axis=0, keepdims=True))
            te = jnp.exp(tl - tm2)
            keep = jnp.exp(tm - tm2)
            ts2 = ts * keep + jnp.sum(te, axis=0, keepdims=True)
            tw2 = tw * keep + jnp.sum(te * (tl - sl), axis=0, keepdims=True)
            ss2 = ss * jnp.exp(sm - sm2) + jnp.sum(jnp.exp(sl - sm2), axis=0, keepdims=True)
            return tm2, ts2, tw2, sm2, ss2

        low_row = jnp.full((1, 256), -1e30, F32)
        zero = jnp.zeros((1, 256), F32)
        stats = lax.fori_loop(0, 2, chunk, (low_row, zero, zero, low_row, zero))
        table = jnp.concatenate(list(stats) + [zero, zero, zero], axis=0)
        st_send[2 * pair] = table[:, :128]
        st_send[2 * pair + 1] = table[:, 128:]

    me = 4 * y + x

    def st_copy(r):
        yy = lax.rem(y + r // 8, 4)
        vv = lax.rem(v + lax.rem(r, 8), 8)
        return remote(
            st_send.at[yy], st_recv.at[c, me], st_ssem.at[r], st_rsem.at[c, me],
            (z * 4 + yy, vv),
        )

    def send_stats(r, carry):
        st_copy(r).start()
        return carry

    lax.fori_loop(1, 32, send_stats, 0)
    cp_st = pltpu.make_async_copy(st_send.at[y], st_recv.at[c, me], load_sem.at[8])
    cp_st.start()
    cp_st.wait()

    def wait_stats(r, carry):
        cc, k = r // 16, lax.rem(r, 16)

        @pl.when(jnp.logical_not((cc == c) & (k == me)))
        def _():
            remote(
                st_send.at[0], st_recv.at[cc, k], st_ssem.at[0], st_rsem.at[cc, k],
                at(z, y, x, mate),
            ).wait_recv()

        return carry

    lax.fori_loop(0, 32, wait_stats, 0)
    for cc in (0, 1):
        pieces = st_recv[cc]
        tm, sm = pieces[:, 0], pieces[:, 3]
        tmax = jnp.max(tm, axis=0, keepdims=True)
        smax = jnp.max(sm, axis=0, keepdims=True)
        tk, sk = jnp.exp(tm - tmax), jnp.exp(sm - smax)
        ts = jnp.sum(pieces[:, 1] * tk, axis=0, keepdims=True)
        tw = jnp.sum(pieces[:, 2] * tk, axis=0, keepdims=True)
        ss = jnp.sum(pieces[:, 4] * sk, axis=0, keepdims=True)
        o_ref[cc : cc + 1, :] = tw / ts - tmax - jnp.log(ts) + smax + jnp.log(ss)

    rw1.wait_send()
    rw2.wait_send()

    @pl.when(home != c)
    def _():
        disp(e).wait_send()

    def sent_rows(r, carry):
        disp(lax.rem(e + r, 32)).wait_send()
        return carry

    lax.fori_loop(1, 32, sent_rows, 0)
    for k in range(6):
        xcopy(x, 0, k, xr).wait_send()
        rs(k, xr).wait_send()

    def sent_back(r, carry):
        for cc in (0, 1):
            b = c * 16 + lax.rem(e + r, 16)

            @pl.when(jnp.logical_not((b == e) & (cc == c)))
            def _():
                comb(b, cc).wait_send()

        return carry

    lax.fori_loop(0, 16, sent_back, 0)
    swap.wait_send()
    for axis in both:
        first(axis, 0, 0, 1).wait_send()
        first(axis, 1, 0, -1).wait_send()
        first(axis, 2, -1, 1, halves[0]).wait_send()
        first(axis, 3, 1, -1, halves[1]).wait_send()
        for k in range(4, 16):
            hop(axis, axis, x, y, k, 1).wait_send()
    for k in range(4):
        ring_up(z, k, k < 3).wait_send()
        ring_down(z, k, k < 3).wait_send()
    for k in range(8):
        to_mate(z, c, k).wait_send()

    def sent_stats(r, carry):
        st_copy(r).wait_send()
        return carry

    lax.fori_loop(1, 32, sent_stats, 0)


def local(
    tokens, teacher_expert, student_expert, priority, expert_in, expert_out,
    teacher_gain, student_gain, teacher_head, student_head,
):
    dma = pltpu.SemaphoreType.DMA
    vm = pltpu.VMEM
    whole = pl.BlockSpec(memory_space=pltpu.VMEM)
    out = pl.pallas_call(
        kernel,
        out_shape=jax.ShapeDtypeStruct((2, 128), F32),
        in_specs=[
            pl.BlockSpec(memory_space=pl.ANY), whole, whole, whole,
            pl.BlockSpec(memory_space=pl.ANY), pl.BlockSpec(memory_space=pl.ANY),
            whole, whole,
            pl.BlockSpec(memory_space=pl.ANY), pl.BlockSpec(memory_space=pl.ANY),
        ],
        out_specs=whole,
        scratch_shapes=[
            vm((256, 256), BF),
            vm((96, 8, 256), BF),
            vm((4, 2, 48, 8, 256), BF),
            vm((2, 2048, 1024), BF),
            vm((2, 1024, 2048), BF),
            vm((2, 384, 1024), F32),
            vm((2, 384, 1024), BF),
            vm((6, 384, 256), BF),
            vm((6, 384, 256), BF),
            vm((2, 384, 256), F32),
            vm((2, 48, 8, 256), BF),
            vm((96, 8, 256), BF),
            vm((2, 272, 256), BF),
            vm((4, 4, 2, 272, 256), BF),
            vm((8, 2, 2, 64, 2048), BF),
            vm((4, 8, 128), F32),
            vm((2, 16, 8, 128), F32),
            vm((512, 768), BF),
            dma((9,)),
            dma((2,)), dma((2,)),
            dma((32,)), dma((16, 2)),
            dma((6,)), dma((6,)),
            dma((6,)), dma((6,)),
            dma((2, 16)), dma((32,)),
            dma((1,)), dma((1,)),
            dma((2, 16)), dma((2, 16)),
            dma((2, 4)), dma((2, 4)),
            dma((8,)), dma((8,)),
            dma((32,)), dma((2, 16)),
        ],
        compiler_params=pltpu.CompilerParams(
            has_side_effects=True, vmem_limit_bytes=64 * 1024 * 1024 - 65536
        ),
    )(
        tokens,
        teacher_expert.reshape(1, -1),
        student_expert.reshape(1, -1),
        priority,
        expert_in,
        expert_out,
        teacher_gain.reshape(1, -1),
        student_gain.reshape(1, -1),
        teacher_head,
        student_head,
    )
    return out.reshape(256)


def solution(mesh):
    placed = (
        P("expert", None),
        P("expert", None),
        P("expert", None),
        P("expert", None),
        P("expert", None, "vocab"),
        P("expert", "vocab", None),
        P(),
        P(),
        P(("vocab", "expert"), None),
        P(("vocab", "expert"), None),
    )
    return jax.shard_map(local, mesh=mesh, in_specs=placed, out_specs=P("expert"), check_vma=False)
```

time: 241 us -> 126 us (0.52)
  Pallas kernels: 0 us -> 124 us
  blocking collectives: 105 us -> 0 us
  waiting for transfers between devices: 39.6 us -> 0 us
  local copies, waits for them, and re-layouts: 33.5 us -> 1.24 us
  matrix products: 19.6 us -> 0 us
  other arithmetic: 15.7 us -> 0 us
  between operations: 13.8 us -> 0.01 us
  starting transfers between devices: 12.4 us -> 0 us
    pallas_call x0 -> x1, Pallas kernels: none -> 124 us  [local(): pl.pallas_call(kernel, out_shape=jax.ShapeDtypeStruct((2, 128), F32), in_...]
    all_to_all x6 -> x0, blocking collectives: 105 us -> none  [the longest x1 39.9 us: sum_in_two_steps(): lax.all_to_all(nearer, far, split_axis=0, concat_axis=0, tiled=True)]
    all_to_all x3 -> x0, waiting for transfers between devices: 39.6 us -> none  [the longest x2 24.2 us: copy_for_each(): lax.all_to_all(jnp.broadcast_to(array[None], (count, *array.shape)), axis...]
    dot_general x4 -> x0, matrix products: 19.6 us -> none  [the longest x1 6.26 us: local(): lax.dot_general(teacher_normed, pieces[0], (((1,), (1,)), ((), ())), pref...]
    all_to_all x3 -> x0, starting transfers between devices: 12.4 us -> none  [the longest x2 7.84 us: copy_for_each(): lax.all_to_all(jnp.broadcast_to(array[None], (count, *array.shape)), axis...]
    reduce_sum x5 -> x0, other arithmetic: 8.52 us -> none  [the longest x1 3.76 us: sum_at_owner(): return arrived.sum(axis=0)]
    gather x3 -> x0, local copies, waits for them, and re-layouts: 6.58 us -> none  [the longest x1 4.27 us: local(): outgoing = padded[owners].reshape(experts, capacity, width)]
    dot_general x1 -> x0, local copies, waits for them, and re-layouts: 6.41 us -> none  [local(): jnp.einsum('nkf,fd->nkd', hidden, weight_out, preferred_element_type=jnp....]
  transfers between devices with their start and end apart: 4 -> 0, of which waited for: 3 -> 0; matrix products, arithmetic and copies ran while one was open for 21% -> 0% of each run, Pallas kernels for 0% -> 0%
where the time goes in v1:
time: 126 us; the launch traced here: 125 us
  Pallas kernels  124 us (98%)
    pallas_call x1, Pallas kernels, local(): pl.pallas_call(kernel, out_shape=jax.ShapeDtypeStruct((2, 128), F32), in_...  124 us

profile of v1, /device:TPU:1, one launch (start us, length us, event | category | flops | bytes accessed | tf_op | source)
XLA Modules:
  0.0 125.4 jit_solution(8672495494723861818)
XLA Ops:
  0.0 124.2 %shard_map.100 = f32[2,128]{1,0:T(2,128)} custom-call(bf16[256,2048]{1,0:T(8,128)(2,1)} %tok_hbm.1, s32[1,256]{1,0:T(1,128)} %bitcast.8, s32[1,256]{1,0:T(1,128)} %bitcast.9, s32[1,256]{1,0:T(1,128)} %pr_ref.1, bf16[1,2048,1024]{2,1,0:T(8,128)(2,1)} %win_hbm.1, bf16[1,1024,2048]{2,1,0:T(8,128)(2,1)} %wout_hbm.1, f32[1,2048]{1,0:T(1,128)} %bitcast.5, ...), custom_call_target="tpu_custom_call" | custom-call | tf_op jit(solution)/shard_map/pallas_call | solution.py:556
  124.2 1.2 copy.12

commit v2 on v1

--- a/solution.py
+++ b/solution.py
@@ -19,7 +19,7 @@
 def kernel(
     tok_hbm, te_ref, se_ref, pr_ref, win_hbm, wout_hbm, tg_ref, sg_ref, th_hbm, sh_hbm,
     o_ref,
-    tok, out_rows, feats, w1, w2, acc, hid, part_send, part_recv, own_part,
+    tok, out_rows, feats, w1, w2, acc, hid, part_send, part_recv, own_part, xin,
     back, ret, unit, units, heads, st_send, st_recv, pick,
     load_sem, w_send, w_recv, disp_send, disp_recv, xag_send, xag_recv,
     rs_send, rs_recv, comb_send, comb_recv, pair_send, pair_recv,
@@ -46,17 +46,35 @@
             device_id=dev, device_id_type=MESH,
         )
 
+    barrier = pltpu.get_barrier_semaphore()
+
+    def greet(ee, vv):
+        @pl.when(jnp.logical_not((ee == e) & (vv == v)))
+        def _():
+            pl.semaphore_signal(barrier, inc=1, device_id=(ee, vv), device_id_type=MESH)
+
+    def greet_rows(r, carry):
+        far = lax.rem(e + 16 + r, 32)
+        greet(far, x * 2 + home)
+        greet(c * 16 + lax.rem(e + r, 16), x * 2 + r // 16)
+        greet(z * 4 + r // 8, lax.rem(r, 8))
+        return carry
+
+    lax.fori_loop(0, 32, greet_rows, 0)
+    greet(step(z, 1, 8) * 4 + y, v)
+    greet(step(z, -1, 8) * 4 + y, v)
+
     cp_tok = pltpu.make_async_copy(
         tok_hbm.at[:, pl.ds(pl.multiple_of(v * 256, 256), 256)], tok, load_sem.at[0]
     )
     cp_tok.start()
+    mine_w2 = pl.ds(pl.multiple_of(c * 1024, 1024), 1024)
     cp_w1 = pltpu.make_async_copy(win_hbm.at[0], w1.at[c], load_sem.at[1])
-    cp_w2 = pltpu.make_async_copy(wout_hbm.at[0], w2.at[c], load_sem.at[2])
+    cp_w2 = pltpu.make_async_copy(wout_hbm.at[0], w2.at[mine_w2], load_sem.at[2])
     cp_th = pltpu.make_async_copy(th_hbm, heads.at[z, c, 0], load_sem.at[3])
     cp_sh = pltpu.make_async_copy(sh_hbm, heads.at[z, c, 1], load_sem.at[4])
     rw1 = remote(win_hbm.at[0], w1.at[c], w_send.at[0], w_recv.at[0], at(z, y, x, mate))
-    rw2 = remote(wout_hbm.at[0], w2.at[c], w_send.at[1], w_recv.at[1], at(z, y, x, mate))
-    rw1.start()
+    rw2 = remote(wout_hbm.at[0], w2.at[mine_w2], w_send.at[1], w_recv.at[1], at(z, y, x, mate))
     cp_w1.start()
 
     def spread(row):
@@ -87,6 +105,7 @@
     cp_tok.wait()
     picked = jnp.dot(gather, tok[...], preferred_element_type=F32)
     out_rows[...] = picked.reshape(96, 8, 256).astype(BF)
+    pl.semaphore_wait(barrier, jnp.where(home == c, 95, 97))
 
     my_slot = pl.ds(3 * lax.rem(e, 16), 3)
 
@@ -113,6 +132,7 @@
         return carry
 
     lax.fori_loop(1, 32, send_rows, 0)
+    rw1.start()
     rw2.start()
     cp_w2.start()
     cp_th.start()
@@ -172,28 +192,30 @@
     cp_w1.wait()
     rw1.wait_recv()
 
-    def rows_of(xx):
-        return [
-            feats[xx, cc].astype(F32).reshape(384, 256).astype(BF) for cc in (0, 1)
-        ]
+    def flatten(xx):
+        xin[xx] = jnp.concatenate(
+            [feats[xx, cc].astype(F32).reshape(384, 256).astype(BF) for cc in (0, 1)], axis=1
+        )
 
     def hidden_pass(xs, first, last):
-        for cc in (0, 1):
-            def body(n, carry):
-                cols = pl.ds(pl.multiple_of(n * 256, 256), 256)
-                total = None if first else acc[cc, :, cols]
-                for xx in xs:
-                    left = jnp.concatenate(rows_of(xx), axis=1)
-                    k = pl.ds(pl.multiple_of(xx * 512, 512), 512)
-                    term = jnp.dot(left, w1[cc, k, cols], preferred_element_type=F32)
-                    total = term if total is None else total + term
-                if last:
-                    hid[cc, :, cols] = gelu(total).astype(BF)
-                else:
-                    acc[cc, :, cols] = total
-                return carry
-
-            lax.fori_loop(0, 4, body, 0)
+        for xx in xs:
+            flatten(xx)
+
+        def body(n, carry):
+            cc, m = n // 2, lax.rem(n, 2)
+            cols = pl.ds(pl.multiple_of(m * 512, 512), 512)
+            total = None if first else acc[cc, :, cols]
+            for xx in xs:
+                k = pl.ds(pl.multiple_of(xx * 512, 512), 512)
+                term = jnp.dot(xin[xx], w1[cc, k, cols], preferred_element_type=F32)
+                total = term if total is None else total + term
+            if last:
+                hid[:, pl.ds(pl.multiple_of(n * 512, 512), 512)] = gelu(total).astype(BF)
+            else:
+                acc[cc, :, cols] = total
+            return carry
+
+        lax.fori_loop(0, 4, body, 0)
 
     hidden_pass([x], True, False)
     xcopy(xl, 0, 0, xr).wait_recv()
@@ -221,36 +243,33 @@
     cp_w2.wait()
     rw2.wait_recv()
 
-    def partial(xx, half):
-        cols = pl.ds(pl.multiple_of(xx * 512 + half * 256, 256), 256)
-        return jnp.dot(hid[0], w2[0, :, cols], preferred_element_type=F32) + jnp.dot(
-            hid[1], w2[1, :, cols], preferred_element_type=F32
-        )
+    def partial(xx):
+        cols = pl.ds(pl.multiple_of(xx * 512, 512), 512)
+        return jnp.dot(hid[...], w2[:, cols], preferred_element_type=F32)
 
     def rs(k, to):
         return remote(
             part_send.at[k], part_recv.at[k], rs_send.at[k], rs_recv.at[k], at(z, y, to, c)
         )
 
-    part_send[0] = partial(xo, 0).astype(BF)
+    far = partial(xo).astype(BF)
+    part_send[0] = far[:, :256]
+    part_send[1] = far[:, 256:]
     rs(0, xr).start()
-    part_send[1] = partial(xo, 1).astype(BF)
     rs(1, xl).start()
-    part_send[2] = partial(xr, 1).astype(BF)
+    own_part[1] = partial(xr)
+    part_send[2] = own_part[1, :, 256:].astype(BF)
     rs(2, xr).start()
-    part_send[3] = partial(xl, 0).astype(BF)
+    own_part[2] = partial(xl)
+    part_send[3] = own_part[2, :, :256].astype(BF)
     rs(3, xl).start()
-    mine = partial(xr, 0)
+    own_part[0] = partial(x)
     rs(0, xr).wait_recv()
-    part_send[4] = (mine + part_recv[0].astype(F32)).astype(BF)
+    part_send[4] = (own_part[1, :, :256] + part_recv[0].astype(F32)).astype(BF)
     rs(4, xr).start()
-    mine = partial(xl, 1)
     rs(1, xl).wait_recv()
-    part_send[5] = (mine + part_recv[1].astype(F32)).astype(BF)
+    part_send[5] = (own_part[2, :, 256:] + part_recv[1].astype(F32)).astype(BF)
     rs(5, xl).start()
-    own_part[0] = partial(x, 0)
-    own_part[1] = partial(x, 1)
-    ring_next(2)
     rs(2, xr).wait_recv()
     rs(3, xl).wait_recv()
 
@@ -273,11 +292,11 @@
         lax.fori_loop(0, 16, one, 0)
 
     rs(4, xr).wait_recv()
-    total = own_part[0] + part_recv[3].astype(F32) + part_recv[4].astype(F32)
+    total = own_part[0, :, :256] + part_recv[3].astype(F32) + part_recv[4].astype(F32)
     back[0] = total.reshape(48, 8, 256).astype(BF)
     send_back(0)
     rs(5, xl).wait_recv()
-    total = own_part[1] + part_recv[2].astype(F32) + part_recv[5].astype(F32)
+    total = own_part[0, :, 256:] + part_recv[2].astype(F32) + part_recv[5].astype(F32)
     back[1] = total.reshape(48, 8, 256).astype(BF)
     send_back(1)
     cp_back = pltpu.make_async_copy(
@@ -300,7 +319,7 @@
         return carry
 
     lax.fori_loop(0, 32, wait_back, 0)
-    ring_next(3)
+    ring_next(2)
 
     rows = ret[...].astype(F32).reshape(768, 256).astype(BF)
     stream = tok[...].astype(F32)
@@ -393,6 +412,8 @@
                 second(axis, rel, -1, 2, 1).start()
             else:
                 second(axis, rel, 1, 2, -1).start()
+        if rel == 3:
+            ring_next(3)
     ring_up(step(z, 4, 8), 3, False).wait_recv()
     ring_down(step(z, 4, 8), 3, False).wait_recv()
     to_mate(step(z, 4, 8), c, 7).start()
@@ -568,12 +589,13 @@
             vm((96, 8, 256), BF),
             vm((4, 2, 48, 8, 256), BF),
             vm((2, 2048, 1024), BF),
-            vm((2, 1024, 2048), BF),
+            vm((2048, 2048), BF),
             vm((2, 384, 1024), F32),
-            vm((2, 384, 1024), BF),
+            vm((384, 2048), BF),
             vm((6, 384, 256), BF),
             vm((6, 384, 256), BF),
-            vm((2, 384, 256), F32),
+            vm((3, 384, 512), F32),
+            vm((4, 384, 512), BF),
             vm((2, 48, 8, 256), BF),
             vm((96, 8, 256), BF),
             vm((2, 272, 256), BF),
@@ -595,7 +617,7 @@
             dma((32,)), dma((2, 16)),
         ],
         compiler_params=pltpu.CompilerParams(
-            has_side_effects=True, vmem_limit_bytes=64 * 1024 * 1024 - 65536
+            has_side_effects=True, collective_id=0, vmem_limit_bytes=64 * 1024 * 1024 - 65536
         ),
     )(
         tokens,

time: 126 us -> 111 us (0.88)
  Pallas kernels: 124 us -> 110 us
    pallas_call x1, Pallas kernels: 124 us -> 110 us  [local(): pl.pallas_call(kernel, out_shape=jax.ShapeDtypeStruct((2, 128), F32), in_...]
where the time goes in v2:
time: 111 us
  Pallas kernels  110 us (99%)
  local copies, waits for them, and re-layouts  1.24 us (1%)
    pallas_call x1, Pallas kernels, local(): pl.pallas_call(kernel, out_shape=jax.ShapeDtypeStruct((2, 128), F32), in_...  110 us

profile of v2, /device:TPU:1, one launch (start us, length us, event | category | flops | bytes accessed | tf_op | source)
XLA Modules:
  0.0 111.2 jit_solution(7575314156423258075)
XLA Ops:
  0.0 110.0 %shard_map.100 = f32[2,128]{1,0:T(2,128)} custom-call(bf16[256,2048]{1,0:T(8,128)(2,1)} %tok_hbm.1, s32[1,256]{1,0:T(1,128)} %bitcast.8, s32[1,256]{1,0:T(1,128)} %bitcast.9, s32[1,256]{1,0:T(1,128)} %pr_ref.1, bf16[1,2048,1024]{2,1,0:T(8,128)(2,1)} %win_hbm.1, bf16[1,1024,2048]{2,1,0:T(8,128)(2,1)} %wout_hbm.1, f32[1,2048]{1,0:T(1,128)} %bitcast.5, ...), custom_call_target="tpu_custom_call" | custom-call | tf_op jit(solution)/shard_map/pallas_call | solution.py:577
  110.0 1.2 %copy.12 = f32[256]{0:T(256)} copy(f32[256]{0:T(256)} %bitcast.7) | data formatting | bytes 2048

commit v3 on v2

v3 whole, which is shorter than its diff:
```python
import jax
import jax.numpy as jnp
from jax import lax
from jax.experimental import pallas as pl
from jax.experimental.pallas import tpu as pltpu
from jax.sharding import PartitionSpec as P

MESH = pl.DeviceIdType.MESH
BF = jnp.bfloat16
F32 = jnp.float32
CAP = 24
NT = (((1,), (1,)), ((), ()))


def gelu(v):
    return 0.5 * v * (1.0 + jnp.tanh(0.7978845608028654 * (v + 0.044715 * v * v * v)))


def kernel(
    tok_hbm, te_hbm, se_hbm, pr_hbm, win_hbm, wout_hbm, tg_hbm, sg_hbm, th_hbm, sh_hbm,
    o_ref,
    ids, gains,
    tok, out_rows, feats, w1, w2, acc, hid, part_send, part_recv, own_part, xin,
    back, ret, unit, units, heads, st_send, st_recv, pick, factor,
    load_sem, w_send, w_recv, disp_send, disp_recv, xag_send, xag_recv,
    rs_send, rs_recv, comb_send, comb_recv, pair_send, pair_recv,
    ag_send, ag_recv, hd_send, hd_recv, hp_send, hp_recv, st_ssem, st_rsem,
):
    e = lax.axis_index("expert")
    v = lax.axis_index("vocab")
    z, y = e // 4, e % 4
    x, c = v // 2, v % 2
    mate = 1 - c
    home = e // 16

    def at(zz, yy, xx, cc):
        return (zz * 4 + yy, xx * 2 + cc)

    def step(a, d, n):
        return lax.rem(a + d + n, n)

    xr, xl, xo = step(x, 1, 4), step(x, -1, 4), step(x, 2, 4)

    def remote(src, dst, ssem, rsem, dev):
        return pltpu.make_async_remote_copy(
            src_ref=src, dst_ref=dst, send_sem=ssem, recv_sem=rsem,
            device_id=dev, device_id_type=MESH,
        )

    cp_tok = pltpu.make_async_copy(
        tok_hbm.at[:, pl.ds(pl.multiple_of(v * 256, 256), 256)], tok, load_sem.at[0]
    )
    cp_ids = [
        pltpu.make_async_copy(src, ids.at[k], load_sem.at[5 + k])
        for k, src in enumerate((te_hbm, se_hbm, pr_hbm))
    ]
    cols = pl.ds(pl.multiple_of(v * 256, 256), 256)
    cp_gains = [
        pltpu.make_async_copy(src.at[:, cols], gains.at[k], load_sem.at[8 + k])
        for k, src in enumerate((tg_hbm, sg_hbm))
    ]
    for cp in cp_ids:
        cp.start()
    cp_tok.start()
    for cp in cp_gains:
        cp.start()
    mine_w2 = pl.ds(pl.multiple_of(c * 1024, 1024), 1024)
    cp_w1 = pltpu.make_async_copy(win_hbm.at[0], w1.at[c], load_sem.at[1])
    cp_w2 = pltpu.make_async_copy(wout_hbm.at[0], w2.at[mine_w2], load_sem.at[2])
    cp_th = pltpu.make_async_copy(th_hbm, heads.at[z, c, 0], load_sem.at[3])
    cp_sh = pltpu.make_async_copy(sh_hbm, heads.at[z, c, 1], load_sem.at[4])
    rw1 = remote(win_hbm.at[0], w1.at[c], w_send.at[0], w_recv.at[0], at(z, y, x, mate))
    rw2 = remote(wout_hbm.at[0], w2.at[mine_w2], w_send.at[1], w_recv.at[1], at(z, y, x, mate))

    barrier = pltpu.get_barrier_semaphore()

    def greet(ee, vv):
        @pl.when(jnp.logical_not((ee == e) & (vv == v)))
        def _():
            pl.semaphore_signal(barrier, inc=1, device_id=(ee, vv), device_id_type=MESH)

    def greet_rows(r, carry):
        far = lax.rem(e + 16 + r, 32)
        greet(far, x * 2 + home)
        greet(c * 16 + lax.rem(e + r, 16), x * 2 + r // 16)
        greet(z * 4 + r // 8, lax.rem(r, 8))
        return carry

    lax.fori_loop(0, 32, greet_rows, 0)
    greet(step(z, 1, 8) * 4 + y, v)
    greet(step(z, -1, 8) * 4 + y, v)

    cp_w1.start()
    for cp in cp_ids:
        cp.wait()

    def spread(row):
        return jnp.broadcast_to(row.astype(F32), (256, 256))

    pj = spread(ids[2])
    pi = pj.T

    def places(expert, lane):
        ej = spread(expert)
        ei = ej.T
        same = ei == ej
        rank_row = jnp.sum(jnp.where(same & (pi < pj), 1.0, 0.0), axis=0, keepdims=True)
        rank_col = jnp.sum(jnp.where(same & (pj < pi), 1.0, 0.0), axis=1, keepdims=True)

        def place(expert, rank):
            return jnp.where(rank < CAP, (2.0 * expert + lane) * CAP + rank, -1.0)

        return place(ej[:1], rank_row), place(ei[:, :1], rank_col)

    t_row, t_col = places(ids[0], 0.0)
    s_row, s_col = places(ids[1], 1.0)
    slot = lax.broadcasted_iota(jnp.int32, (768, 256), 0).astype(F32)
    gather = jnp.where((slot == t_row) | (slot == s_row), 1.0, 0.0).astype(BF)
    lanes = lax.broadcasted_iota(jnp.int32, (256, 768), 1).astype(F32)
    pick[0:256] = jnp.where(lanes == t_col, 1.0, 0.0).astype(BF)
    pick[256:512] = jnp.where(lanes == s_col, 1.0, 0.0).astype(BF)
    cp_tok.wait()
    for cp in cp_gains:
        cp.wait()
    picked = jnp.dot(gather, tok[...], preferred_element_type=F32)
    out_rows[0] = picked[:, :128].reshape(96, 8, 128).astype(BF)
    out_rows[1] = picked[:, 128:].reshape(96, 8, 128).astype(BF)
    pl.semaphore_wait(barrier, jnp.where(home == c, 95, 97))

    my_slot = pl.ds(3 * lax.rem(e, 16), 3)

    def disp(to, h):
        return remote(
            out_rows.at[h, pl.ds(3 * to, 3)], feats.at[x, c, h, my_slot],
            disp_send.at[h], disp_recv.at[h], (to, x * 2 + home),
        )

    cp_self = [
        pltpu.make_async_copy(
            out_rows.at[h, pl.ds(3 * e, 3)], feats.at[x, c, h, my_slot], disp_recv.at[h]
        )
        for h in (0, 1)
    ]

    for h in (0, 1):

        @pl.when(home == c)
        def _():
            cp_self[h].start()

        @pl.when(home != c)
        def _():
            disp(e, h).start()

        def send_rows(r, carry):
            disp(lax.rem(e + r, 32), h).start()
            return carry

        lax.fori_loop(1, 32, send_rows, 0)
    rw1.start()
    rw2.start()
    cp_w2.start()
    cp_th.start()
    cp_sh.start()

    def wait_rows(h):
        here = feats.at[x, :, h]
        remote(
            here, here, disp_send.at[h], disp_recv.at[h], at(z, y, x, mate)
        ).wait_recv()

    def xcopy(xx, cc, h, k, to):
        piece = feats.at[xx, cc, h]
        return remote(piece, piece, xag_send.at[0], xag_recv.at[h, k], at(z, y, to, c))

    for h in (0, 1):
        wait_rows(h)
        xcopy(x, 0, h, 0, xr).start()
        xcopy(x, 1, h, 1, xl).start()
        xcopy(x, 1, h, 2, xr).start()
        xcopy(x, 0, h, 3, xl).start()

    zu, zd = step(z, 1, 8), step(z, -1, 8)
    cp_th.wait()
    cp_sh.wait()

    def ring_up(zz, k, both):
        piece = heads.at[zz, c] if both else heads.at[zz, c, 0]
        return remote(piece, piece, hd_send.at[0], hd_recv.at[0, k], at(zu, y, x, c))

    def ring_down(zz, k, both):
        piece = heads.at[zz, c] if both else heads.at[zz, c, 1]
        return remote(piece, piece, hd_send.at[0], hd_recv.at[1, k], at(zd, y, x, c))

    def to_mate(zz, cc, k):
        piece = heads.at[zz, cc]
        return remote(piece, piece, hp_send.at[0], hp_recv.at[k], at(z, y, x, mate))

    ring_up(z, 0, True).start()
    ring_down(z, 0, True).start()
    to_mate(z, c, 0).start()

    cp_w1.wait()
    rw1.wait_recv()

    def flatten(xx):
        xin[xx] = jnp.concatenate(
            [
                feats[xx, cc, h].astype(F32).reshape(384, 128).astype(BF)
                for cc in (0, 1)
                for h in (0, 1)
            ],
            axis=1,
        )

    def hidden_pass(xs, first, last):
        for xx in xs:
            flatten(xx)

        def body(n, carry):
            cc, m = n // 2, lax.rem(n, 2)
            cols = pl.ds(pl.multiple_of(m * 512, 512), 512)
            total = None if first else acc[cc, :, cols]
            for xx in xs:
                k = pl.ds(pl.multiple_of(xx * 512, 512), 512)
                term = jnp.dot(xin[xx], w1[cc, k, cols], preferred_element_type=F32)
                total = term if total is None else total + term
            if last:
                hid[:, pl.ds(pl.multiple_of(n * 512, 512), 512)] = gelu(total).astype(BF)
            else:
                acc[cc, :, cols] = total
            return carry

        lax.fori_loop(0, 4, body, 0)

    hidden_pass([x], True, False)
    for h in (0, 1):
        xcopy(xl, 0, h, 0, xr).wait_recv()
        xcopy(xl, 0, h, 4, xr).start()
        xcopy(xr, 1, h, 1, xl).wait_recv()
        xcopy(xr, 1, h, 5, xl).start()
        xcopy(xl, 1, h, 2, xr).wait_recv()
        xcopy(xr, 0, h, 3, xl).wait_recv()
    hidden_pass([xl, xr], False, False)
    for h in (0, 1):
        xcopy(xo, 0, h, 4, xr).wait_recv()
        xcopy(xo, 1, h, 5, xl).wait_recv()

    def ring_next(k):
        lo, hi = step(z, -k, 8), step(z, k, 8)
        ring_up(lo, k - 1, True).wait_recv()
        ring_down(hi, k - 1, True).wait_recv()
        ring_up(lo, k, k < 3).start()
        ring_down(hi, k, k < 3).start()
        to_mate(lo, c, 1).start()
        to_mate(hi, c, 0).start()

    ring_next(1)
    hidden_pass([xo], False, True)

    cp_w2.wait()
    rw2.wait_recv()

    def partial(xx):
        cols = pl.ds(pl.multiple_of(xx * 512, 512), 512)
        return jnp.dot(hid[...], w2[:, cols], preferred_element_type=F32)

    def rs(h, k, to):
        return remote(
            part_send.at[h, k], part_recv.at[h, k], rs_send.at[0], rs_recv.at[h, k],
            at(z, y, to, c),
        )

    far = partial(xo).astype(BF)
    for h in (0, 1):
        part_send[h, 0] = far[:192, 256 * h : 256 * h + 256]
        part_send[h, 1] = far[192:, 256 * h : 256 * h + 256]
    rs(0, 0, xr).start()
    rs(0, 1, xl).start()
    own_part[1] = partial(xr)
    for h in (0, 1):
        part_send[h, 2] = own_part[1, 192:, 256 * h : 256 * h + 256].astype(BF)
    rs(0, 2, xr).start()
    own_part[2] = partial(xl)
    for h in (0, 1):
        part_send[h, 3] = own_part[2, :192, 256 * h : 256 * h + 256].astype(BF)
    rs(0, 3, xl).start()

    def merge(h):
        half = slice(256 * h, 256 * h + 256)
        rs(h, 0, xr).wait_recv()
        part_send[h, 4] = (own_part[1, :192, half] + part_recv[h, 0].astype(F32)).astype(BF)
        rs(h, 4, xr).start()
        rs(h, 1, xl).wait_recv()
        part_send[h, 5] = (own_part[2, 192:, half] + part_recv[h, 1].astype(F32)).astype(BF)
        rs(h, 5, xl).start()

    merge(0)
    rs(1, 0, xr).start()
    rs(1, 1, xl).start()
    rs(1, 2, xr).start()
    rs(1, 3, xl).start()
    own_part[0] = partial(x)

    def comb(b, cc):
        return remote(
            back.at[cc, pl.ds(3 * lax.rem(b, 16), 3)], ret.at[pl.ds(3 * e, 3)],
            comb_send.at[cc], comb_recv.at[0], (b, x * 2 + cc),
        )

    def send_back(cc):
        def one(r, carry):
            b = c * 16 + lax.rem(e + r, 16)

            @pl.when(jnp.logical_not((b == e) & (cc == c)))
            def _():
                comb(b, cc).start()

            return carry

        lax.fori_loop(0, 16, one, 0)

    def collect(h):
        half = slice(256 * h, 256 * h + 256)
        for rows_, near, merged in ((slice(0, 192), 3, 4), (slice(192, 384), 2, 5)):
            rs(h, near, xr).wait_recv()
            rs(h, merged, xr).wait_recv()
            total = (
                own_part[0, rows_, half]
                + part_recv[h, near].astype(F32)
                + part_recv[h, merged].astype(F32)
            )
            back[h, rows_.start // 8 : rows_.stop // 8] = total.reshape(24, 8, 256).astype(BF)
        send_back(h)

    collect(0)
    merge(1)
    collect(1)
    cp_back = pltpu.make_async_copy(
        back.at[c, pl.ds(3 * lax.rem(e, 16), 3)], ret.at[pl.ds(3 * e, 3)], comb_recv.at[0]
    )

    @pl.when(home == c)
    def _():
        cp_back.start()

    swap = remote(
        unit, units.at[y, x, c], pair_send.at[0], pair_recv.at[0], at(z, y, x, mate)
    )
    from_mate = remote(
        unit, units.at[y, x, mate], pair_send.at[0], pair_recv.at[0], at(z, y, x, mate)
    )

    def finish(core):
        pltpu.make_async_copy(ret, ret, comb_recv.at[0]).wait()
        rows = ret[...].astype(F32).reshape(768, 256).astype(BF)
        stream = tok[...].astype(F32)
        kept = units.at[y, x, core]
        squares = []
        for k in (0, 1):
            branch = jnp.dot(
                pick[256 * k : 256 * k + 256], rows, preferred_element_type=F32
            )
            summed = stream + branch
            scaled = (summed * gains[k]).astype(BF)
            parts = (scaled[:128], scaled[128:])
            kept[128 * k : 128 * k + 128] = parts[core]
            unit[128 * k : 128 * k + 128] = parts[1 - core]
            column = jnp.sum(summed * summed, axis=1, keepdims=True)
            squares.append(jnp.broadcast_to(column, (256, 128)).T[:1])
        low = lax.broadcasted_iota(jnp.int32, (16, 256), 0) == 0
        for h, place in ((core, kept), (1 - core, unit)):
            lines = []
            for k in (0, 1):
                part = squares[k][:, 128 * h : 128 * h + 128]
                top = part.astype(BF).astype(F32)
                lines.append(
                    jnp.broadcast_to(jnp.concatenate([top, part - top], axis=1), (16, 256))
                )
            place[256:272] = jnp.where(low, lines[0], lines[1]).astype(BF)
        swap.start()

    here = (x, y)

    def place_of(axis, a, b):
        return units.at[b, a, 0] if axis == 0 else units.at[a, b, 1]

    def dev_of(axis, d):
        p, q = (step(x, d, 4), y) if axis == 0 else (x, step(y, d, 4))
        return at(z, q, p, c)

    def hop(axis, along, a, b, k, d, rows_=None):
        piece = place_of(axis, a, b)
        if rows_ is not None:
            piece = piece.at[rows_[0] : rows_[1]]
        return remote(
            piece, piece, ag_send.at[axis, min(k // 4, 1)], ag_recv.at[axis, k], dev_of(along, d)
        )

    halves = ((0, 128), (128, 272))

    def first(axis, k, off, d, rows_=None):
        a = step(here[axis], off, 4)
        return hop(axis, axis, a, here[1 - axis], k, d, rows_)

    def second(axis, rel, off, kind, d):
        a = step(here[axis], rel, 4)
        b = step(here[1 - axis], off, 4)
        return hop(axis, 1 - axis, a, b, 4 + 3 * rel + kind, d)

    both = (0, 1)

    def begin(axis):
        @pl.when(c == axis)
        def _():
            finish(axis)

        @pl.when(c != axis)
        def _():
            from_mate.wait_recv()

        first(axis, 0, 0, 1).start()
        first(axis, 1, 0, -1).start()
        second(axis, 0, 0, 0, 1).start()
        second(axis, 0, 0, 1, -1).start()

    def forward_first(axis):
        first(axis, 0, -1, 1).wait_recv()
        first(axis, 2, -1, 1, halves[0]).start()
        first(axis, 1, 1, -1).wait_recv()
        first(axis, 3, 1, -1, halves[1]).start()

    def pass_on(axis, rel):
        second(axis, rel, 0, 0, 1).start()
        second(axis, rel, 0, 1, -1).start()

    def opposite(axis):
        first(axis, 2, 2, 1, halves[0]).wait_recv()
        first(axis, 3, 2, -1, halves[1]).wait_recv()
        pass_on(axis, 2)

    def forward_second(axis, rel):
        second(axis, rel, -1, 0, 1).wait_recv()
        second(axis, rel, 1, 1, -1).wait_recv()
        if rel in (0, 1):
            second(axis, rel, -1, 2, 1).start()
        else:
            second(axis, rel, 1, 2, -1).start()

    begin(0)
    forward_first(0)
    pass_on(0, 3)
    begin(1)
    ring_next(2)
    pass_on(0, 1)
    forward_first(1)
    pass_on(1, 3)
    pass_on(1, 1)
    opposite(0)
    opposite(1)
    for rel in (0, 3, 1, 2):
        for axis in both:
            forward_second(axis, rel)
        if rel == 3:
            ring_next(3)
    for rel in (0, 3, 1, 2):
        for axis in both:
            second(axis, rel, 2, 2, 1 if rel in (0, 1) else -1).wait_recv()
    ring_up(step(z, 4, 8), 3, False).wait_recv()
    ring_down(step(z, 4, 8), 3, False).wait_recv()
    to_mate(step(z, 4, 8), c, 1).start()

    def from_mate_heads(k):
        pltpu.make_async_copy(heads.at[0:4, 0], heads.at[0:4, 0], hp_recv.at[k]).wait()

    for yy in range(4):
        for k in (0, 1):
            total = jnp.zeros((1, 128), F32)
            for xx in range(4):
                for cc in (0, 1):
                    line = units[yy, xx, cc, 256:272, :].astype(F32)[k : k + 1]
                    total = total + line[:, :128] + line[:, 128:]
            factor[yy, k : k + 1] = lax.rsqrt(total * (1.0 / 2048.0) + 1e-5)

    def logits(pair, k, n):
        left = [heads[lax.rem(z + 4 * n + i, 8), :, k].reshape(128, 2048) for i in range(4)]
        left = jnp.concatenate(left, axis=0)
        total = None
        for xx in range(4):
            for cc in (0, 1):
                right = jnp.concatenate(
                    [
                        units[2 * pair + i, xx, cc, 128 * k : 128 * k + 128, :]
                        for i in (0, 1)
                    ],
                    axis=0,
                )
                kk = (xx * 2 + cc) * 256
                term = lax.dot_general(
                    left[:, kk : kk + 256], right, NT, preferred_element_type=F32
                )
                total = term if total is None else total + term
        scale = [factor[2 * pair + i, k : k + 1] for i in (0, 1)]
        return total * jnp.concatenate(scale, axis=1)

    def chunk(n):
        def one_pair(pair, carry):
            tl = logits(pair, 0, n)
            sl = logits(pair, 1, n)
            tm = jnp.max(tl, axis=0, keepdims=True)
            sm = jnp.max(sl, axis=0, keepdims=True)
            if n == 1:
                old = jnp.concatenate([st_send[2 * pair], st_send[2 * pair + 1]], axis=1)
                tm = jnp.maximum(tm, old[0:1])
                sm = jnp.maximum(sm, old[3:4])
            te = jnp.exp(tl - tm)
            ts = jnp.sum(te, axis=0, keepdims=True)
            tw = jnp.sum(te * (tl - sl), axis=0, keepdims=True)
            ss = jnp.sum(jnp.exp(sl - sm), axis=0, keepdims=True)
            if n == 1:
                keep = jnp.exp(old[0:1] - tm)
                ts = ts + old[1:2] * keep
                tw = tw + old[2:3] * keep
                ss = ss + old[4:5] * jnp.exp(old[3:4] - sm)
            zero = jnp.zeros((3, 256), F32)
            table = jnp.concatenate([tm, ts, tw, sm, ss, zero], axis=0)
            st_send[2 * pair] = table[:, :128]
            st_send[2 * pair + 1] = table[:, 128:]
            return carry

        lax.fori_loop(0, 2, one_pair, 0)

    from_mate_heads(0)
    chunk(0)
    from_mate_heads(1)
    chunk(1)

    me = 4 * y + x

    def st_copy(r):
        yy = lax.rem(y + r // 8, 4)
        vv = lax.rem(v + lax.rem(r, 8), 8)
        return remote(
            st_send.at[yy], st_recv.at[c, me], st_ssem.at[0], st_rsem.at[0],
            (z * 4 + yy, vv),
        )

    def send_stats(r, carry):
        st_copy(r).start()
        return carry

    lax.fori_loop(1, 32, send_stats, 0)
    pltpu.make_async_copy(st_send.at[y], st_recv.at[c, me], st_rsem.at[0]).start()

    rw1.wait_send()
    rw2.wait_send()

    for h in (0, 1):

        @pl.when(home != c)
        def _():
            pltpu.make_async_copy(out_rows.at[h], out_rows.at[h], disp_send.at[h]).wait()

        @pl.when(home == c)
        def _():
            most = out_rows.at[h, pl.ds(0, 93)]
            pltpu.make_async_copy(most, most, disp_send.at[h]).wait()

    pltpu.make_async_copy(feats.at[0:3], feats.at[0:3], xag_send.at[0]).wait()
    pltpu.make_async_copy(part_send, part_send, rs_send.at[0]).wait()

    for h in (0, 1):

        @pl.when((home == c) & (c == h))
        def _():
            most = back.at[h, pl.ds(0, 45)]
            pltpu.make_async_copy(most, most, comb_send.at[h]).wait()

        @pl.when(jnp.logical_not((home == c) & (c == h)))
        def _():
            pltpu.make_async_copy(back.at[h], back.at[h], comb_send.at[h]).wait()

    swap.wait_send()
    for axis in both:
        for k, sent in ((0, units.at[0:3, 0, 0]), (1, units.at[0:3, :, 0])):
            pltpu.make_async_copy(sent, sent, ag_send.at[axis, k]).wait()
    pltpu.make_async_copy(heads.at[0:7, 0], heads.at[0:7, 0], hd_send.at[0]).wait()
    pltpu.make_async_copy(heads.at[:, 0], heads.at[:, 0], hp_send.at[0]).wait()

    pltpu.make_async_copy(st_recv, st_recv, st_rsem.at[0]).wait()
    for cc in (0, 1):
        pieces = st_recv[cc]
        tm, sm = pieces[:, 0], pieces[:, 3]
        tmax = jnp.max(tm, axis=0, keepdims=True)
        smax = jnp.max(sm, axis=0, keepdims=True)
        tk, sk = jnp.exp(tm - tmax), jnp.exp(sm - smax)
        ts = jnp.sum(pieces[:, 1] * tk, axis=0, keepdims=True)
        tw = jnp.sum(pieces[:, 2] * tk, axis=0, keepdims=True)
        ss = jnp.sum(pieces[:, 4] * sk, axis=0, keepdims=True)
        o_ref[cc : cc + 1, :] = tw / ts - tmax - jnp.log(ts) + smax + jnp.log(ss)

    sent = out_rows.at[0, pl.ds(0, 62)]
    pltpu.make_async_copy(sent, sent, st_ssem.at[0]).wait()


def local(
    tokens, teacher_expert, student_expert, priority, expert_in, expert_out,
    teacher_gain, student_gain, teacher_head, student_head,
):
    dma = pltpu.SemaphoreType.DMA
    vm = pltpu.VMEM
    whole = pl.BlockSpec(memory_space=pltpu.VMEM)
    out = pl.pallas_call(
        kernel,
        out_shape=jax.ShapeDtypeStruct((2, 128), F32),
        in_specs=[pl.BlockSpec(memory_space=pl.ANY)] * 10,
        out_specs=whole,
        scratch_shapes=[
            vm((3, 1, 256), jnp.int32),
            vm((2, 1, 256), F32),
            vm((256, 256), BF),
            vm((2, 96, 8, 128), BF),
            vm((4, 2, 2, 48, 8, 128), BF),
            vm((2, 2048, 1024), BF),
            vm((2048, 2048), BF),
            vm((2, 384, 1024), F32),
            vm((384, 2048), BF),
            vm((2, 6, 192, 256), BF),
            vm((2, 6, 192, 256), BF),
            vm((3, 384, 512), F32),
            vm((4, 384, 512), BF),
            vm((2, 48, 8, 256), BF),
            vm((96, 8, 256), BF),
            vm((272, 256), BF),
            vm((4, 4, 2, 272, 256), BF),
            vm((8, 2, 2, 64, 2048), BF),
            vm((4, 8, 128), F32),
            vm((2, 16, 8, 128), F32),
            vm((512, 768), BF),
            vm((4, 8, 128), F32),
            dma((10,)),
            dma((2,)), dma((2,)),
            dma((2,)), dma((2,)),
            dma((1,)), dma((2, 6)),
            dma((1,)), dma((2, 6)),
            dma((2,)), dma((1,)),
            dma((1,)), dma((1,)),
            dma((2, 2)), dma((2, 16)),
            dma((1,)), dma((2, 4)),
            dma((1,)), dma((2,)),
            dma((1,)), dma((1,)),
        ],
        compiler_params=pltpu.CompilerParams(
            has_side_effects=True, collective_id=0, vmem_limit_bytes=64 * 1024 * 1024 - 65536
        ),
    )(
        tokens,
        teacher_expert.reshape(1, -1),
        student_expert.reshape(1, -1),
        priority,
        expert_in,
        expert_out,
        teacher_gain.reshape(1, -1),
        student_gain.reshape(1, -1),
        teacher_head,
        student_head,
    )
    return out.reshape(256)


def solution(mesh):
    placed = (
        P("expert", None),
        P("expert", None),
        P("expert", None),
        P("expert", None),
        P("expert", None, "vocab"),
        P("expert", "vocab", None),
        P(),
        P(),
        P(("vocab", "expert"), None),
        P(("vocab", "expert"), None),
    )
    return jax.shard_map(local, mesh=mesh, in_specs=placed, out_specs=P("expert"), check_vma=False)
```

time: 111 us -> 104 us (0.937)
  Pallas kernels: 110 us -> 102 us
    pallas_call x1, Pallas kernels: 110 us -> 102 us  [local(): pl.pallas_call(kernel, out_shape=jax.ShapeDtypeStruct((2, 128), F32), in_...]
where the time goes in v3:
time: 104 us
  Pallas kernels  102 us (98%)
  local copies, waits for them, and re-layouts  1.24 us (1%)
    pallas_call x1, Pallas kernels, local(): pl.pallas_call(kernel, out_shape=jax.ShapeDtypeStruct((2, 128), F32), in_...  102 us

profile of v3, /device:TPU:1, one launch (start us, length us, event | category | flops | bytes accessed | tf_op | source)
XLA Modules:
  0.0 103.6 jit_solution(3814561589662870143)
XLA Ops:
  0.0 102.4 %shard_map.100 = f32[2,128]{1,0:T(2,128)} custom-call(bf16[256,2048]{1,0:T(8,128)(2,1)} %tok_hbm.1, s32[1,256]{1,0:T(1,128)} %bitcast.8, s32[1,256]{1,0:T(1,128)} %bitcast.9, s32[1,256]{1,0:T(1,128)} %pr_hbm.1, bf16[1,2048,1024]{2,1,0:T(8,128)(2,1)} %win_hbm.1, bf16[1,1024,2048]{2,1,0:T(8,128)(2,1)} %wout_hbm.1, f32[1,2048]{1,0:T(1,128)} %bitcast.5, ...), custom_call_target="tpu_custom_call" | custom-call | tf_op jit(solution)/shard_map/pallas_call | solution.py:613
  102.4 1.2 %copy.12 = f32[256]{0:T(256)} copy(f32[256]{0:T(256)} %bitcast.7) | data formatting | bytes 2048

commit v4 on v3

--- a/solution.py
+++ b/solution.py
@@ -21,7 +21,7 @@
     o_ref,
     ids, gains,
     tok, out_rows, feats, w1, w2, acc, hid, part_send, part_recv, own_part, xin,
-    back, ret, unit, units, heads, st_send, st_recv, pick, factor,
+    back, ret, unit, units, heads, st_send, st_recv, pick, factor, res,
     load_sem, w_send, w_recv, disp_send, disp_recv, xag_send, xag_recv,
     rs_send, rs_recv, comb_send, comb_recv, pair_send, pair_recv,
     ag_send, ag_recv, hd_send, hd_recv, hp_send, hp_recv, st_ssem, st_rsem,
@@ -48,15 +48,15 @@
         )
 
     cp_tok = pltpu.make_async_copy(
-        tok_hbm.at[:, pl.ds(pl.multiple_of(v * 256, 256), 256)], tok, load_sem.at[0]
+        tok_hbm.at[:, pl.ds(pl.multiple_of(v * 256, 256), 256)], tok, load_sem.at[1]
     )
     cp_ids = [
-        pltpu.make_async_copy(src, ids.at[k], load_sem.at[5 + k])
+        pltpu.make_async_copy(src, ids.at[k], load_sem.at[0])
         for k, src in enumerate((te_hbm, se_hbm, pr_hbm))
     ]
     cols = pl.ds(pl.multiple_of(v * 256, 256), 256)
     cp_gains = [
-        pltpu.make_async_copy(src.at[:, cols], gains.at[k], load_sem.at[8 + k])
+        pltpu.make_async_copy(src.at[:, cols], gains.at[k], load_sem.at[2])
         for k, src in enumerate((tg_hbm, sg_hbm))
     ]
     for cp in cp_ids:
@@ -65,10 +65,10 @@
     for cp in cp_gains:
         cp.start()
     mine_w2 = pl.ds(pl.multiple_of(c * 1024, 1024), 1024)
-    cp_w1 = pltpu.make_async_copy(win_hbm.at[0], w1.at[c], load_sem.at[1])
-    cp_w2 = pltpu.make_async_copy(wout_hbm.at[0], w2.at[mine_w2], load_sem.at[2])
-    cp_th = pltpu.make_async_copy(th_hbm, heads.at[z, c, 0], load_sem.at[3])
-    cp_sh = pltpu.make_async_copy(sh_hbm, heads.at[z, c, 1], load_sem.at[4])
+    cp_w1 = pltpu.make_async_copy(win_hbm.at[0], w1.at[c], load_sem.at[3])
+    cp_w2 = pltpu.make_async_copy(wout_hbm.at[0], w2.at[mine_w2], load_sem.at[4])
+    cp_th = pltpu.make_async_copy(th_hbm, heads.at[z, c, 0], load_sem.at[5])
+    cp_sh = pltpu.make_async_copy(sh_hbm, heads.at[z, c, 1], load_sem.at[5])
     rw1 = remote(win_hbm.at[0], w1.at[c], w_send.at[0], w_recv.at[0], at(z, y, x, mate))
     rw2 = remote(wout_hbm.at[0], w2.at[mine_w2], w_send.at[1], w_recv.at[1], at(z, y, x, mate))
 
@@ -91,8 +91,7 @@
     greet(step(z, -1, 8) * 4 + y, v)
 
     cp_w1.start()
-    for cp in cp_ids:
-        cp.wait()
+    pltpu.make_async_copy(ids, ids, load_sem.at[0]).wait()
 
     def spread(row):
         return jnp.broadcast_to(row.astype(F32), (256, 256))
@@ -120,14 +119,15 @@
     pick[0:256] = jnp.where(lanes == t_col, 1.0, 0.0).astype(BF)
     pick[256:512] = jnp.where(lanes == s_col, 1.0, 0.0).astype(BF)
     cp_tok.wait()
-    for cp in cp_gains:
-        cp.wait()
+    pltpu.make_async_copy(gains, gains, load_sem.at[2]).wait()
     picked = jnp.dot(gather, tok[...], preferred_element_type=F32)
     out_rows[0] = picked[:, :128].reshape(96, 8, 128).astype(BF)
     out_rows[1] = picked[:, 128:].reshape(96, 8, 128).astype(BF)
     pl.semaphore_wait(barrier, jnp.where(home == c, 95, 97))
 
     my_slot = pl.ds(3 * lax.rem(e, 16), 3)
+
+    far_first = [lax.rem(z + d, 8) for d in (4, 3, 5, 2, 6, 1, 7, 0)]
 
     def disp(to, h):
         return remote(
@@ -152,11 +152,13 @@
         def _():
             disp(e, h).start()
 
-        def send_rows(r, carry):
-            disp(lax.rem(e + r, 32), h).start()
-            return carry
-
-        lax.fori_loop(1, 32, send_rows, 0)
+        for k, zz in enumerate(far_first):
+
+            def send_rows(r, carry):
+                disp(zz * 4 + lax.rem(y + 1 + r, 4), h).start()
+                return carry
+
+            lax.fori_loop(0, 3 if k == 7 else 4, send_rows, 0)
     rw1.start()
     rw2.start()
     cp_w2.start()
@@ -181,8 +183,7 @@
         xcopy(x, 0, h, 3, xl).start()
 
     zu, zd = step(z, 1, 8), step(z, -1, 8)
-    cp_th.wait()
-    cp_sh.wait()
+    pltpu.make_async_copy(heads.at[z, c], heads.at[z, c], load_sem.at[5]).wait()
 
     def ring_up(zz, k, both):
         piece = heads.at[zz, c] if both else heads.at[zz, c, 0]
@@ -255,8 +256,8 @@
         to_mate(lo, c, 1).start()
         to_mate(hi, c, 0).start()
 
+    hidden_pass([xo], False, True)
     ring_next(1)
-    hidden_pass([xo], False, True)
 
     cp_w2.wait()
     rw2.wait_recv()
@@ -309,16 +310,20 @@
         )
 
     def send_back(cc):
-        def one(r, carry):
-            b = c * 16 + lax.rem(e + r, 16)
-
-            @pl.when(jnp.logical_not((b == e) & (cc == c)))
+        for zz in far_first:
+
+            @pl.when(zz // 4 == c)
             def _():
-                comb(b, cc).start()
-
-            return carry
-
-        lax.fori_loop(0, 16, one, 0)
+                def one(r, carry):
+                    b = zz * 4 + lax.rem(y + 1 + r, 4)
+
+                    @pl.when(jnp.logical_not((b == e) & (cc == c)))
+                    def _():
+                        comb(b, cc).start()
+
+                    return carry
+
+                lax.fori_loop(0, 4, one, 0)
 
     def collect(h):
         half = slice(256 * h, 256 * h + 256)
@@ -381,91 +386,97 @@
         swap.start()
 
     here = (x, y)
-
-    def place_of(axis, a, b):
-        return units.at[b, a, 0] if axis == 0 else units.at[a, b, 1]
-
-    def dev_of(axis, d):
-        p, q = (step(x, d, 4), y) if axis == 0 else (x, step(y, d, 4))
+    spans = ((0, 64, 128), (128, 192, 272))
+
+    def dev_of(along, d):
+        p, q = (step(x, d, 4), y) if along == 0 else (x, step(y, d, 4))
         return at(z, q, p, c)
 
-    def hop(axis, along, a, b, k, d, rows_=None):
-        piece = place_of(axis, a, b)
-        if rows_ is not None:
-            piece = piece.at[rows_[0] : rows_[1]]
+    def hop(axis, half, along, a, b, k, d, ends):
+        xx, yy = (a, b) if axis == 0 else (b, a)
+        piece = units.at[yy, xx, half, ends[0] : ends[1]]
         return remote(
-            piece, piece, ag_send.at[axis, min(k // 4, 1)], ag_recv.at[axis, k], dev_of(along, d)
+            piece, piece, ag_send.at[axis, half, min(k // 4, 1)], ag_recv.at[axis, half, k],
+            dev_of(along, d),
         )
 
-    halves = ((0, 128), (128, 272))
-
-    def first(axis, k, off, d, rows_=None):
+    def first(axis, half, k, off, d):
+        lo, mid, hi = spans[axis]
+        ends = ((lo, hi), (lo, hi), (lo, mid), (mid, hi))[k]
         a = step(here[axis], off, 4)
-        return hop(axis, axis, a, here[1 - axis], k, d, rows_)
-
-    def second(axis, rel, off, kind, d):
+        return hop(axis, half, axis, a, here[1 - axis], k, d, ends)
+
+    def second(axis, half, rel, off, kind, d):
         a = step(here[axis], rel, 4)
         b = step(here[1 - axis], off, 4)
-        return hop(axis, 1 - axis, a, b, 4 + 3 * rel + kind, d)
+        ends = (spans[axis][0], spans[axis][2])
+        return hop(axis, half, 1 - axis, a, b, 4 + (rel if kind == 0 else 4), d, ends)
 
     both = (0, 1)
 
-    def begin(axis):
-        @pl.when(c == axis)
-        def _():
-            finish(axis)
-
-        @pl.when(c != axis)
+    def begin(half):
+        @pl.when(c == half)
+        def _():
+            finish(half)
+
+        @pl.when(c != half)
         def _():
             from_mate.wait_recv()
 
-        first(axis, 0, 0, 1).start()
-        first(axis, 1, 0, -1).start()
-        second(axis, 0, 0, 0, 1).start()
-        second(axis, 0, 0, 1, -1).start()
-
-    def forward_first(axis):
-        first(axis, 0, -1, 1).wait_recv()
-        first(axis, 2, -1, 1, halves[0]).start()
-        first(axis, 1, 1, -1).wait_recv()
-        first(axis, 3, 1, -1, halves[1]).start()
-
-    def pass_on(axis, rel):
-        second(axis, rel, 0, 0, 1).start()
-        second(axis, rel, 0, 1, -1).start()
-
-    def opposite(axis):
-        first(axis, 2, 2, 1, halves[0]).wait_recv()
-        first(axis, 3, 2, -1, halves[1]).wait_recv()
-        pass_on(axis, 2)
-
-    def forward_second(axis, rel):
-        second(axis, rel, -1, 0, 1).wait_recv()
-        second(axis, rel, 1, 1, -1).wait_recv()
-        if rel in (0, 1):
-            second(axis, rel, -1, 2, 1).start()
-        else:
-            second(axis, rel, 1, 2, -1).start()
+        for axis in both:
+            first(axis, half, 0, 0, 1).start()
+            first(axis, half, 1, 0, -1).start()
+        pass_on(half, 0)
+
+    def forward_first(half):
+        for axis in both:
+            first(axis, half, 0, -1, 1).wait_recv()
+            first(axis, half, 2, -1, 1).start()
+            first(axis, half, 1, 1, -1).wait_recv()
+            first(axis, half, 3, 1, -1).start()
+
+    def pass_on(half, rel):
+        for axis in both:
+            second(axis, half, rel, 0, 0, 1).start()
+            second(axis, half, rel, 0, 0, -1).start()
+
+    def opposite(half):
+        for axis in both:
+            first(axis, half, 2, 2, 1).wait_recv()
+            first(axis, half, 3, 2, -1).wait_recv()
+        pass_on(half, 2)
+
+    def forward_second(half, rel):
+        for axis in both:
+            pair_of = units.at[0:2, 0, 0, spans[axis][0] : spans[axis][2]]
+            pltpu.make_async_copy(
+                pair_of, pair_of, ag_recv.at[axis, half, 4 + rel]
+            ).wait()
+            if rel in (0, 1):
+                second(axis, half, rel, -1, 1, 1).start()
+            else:
+                second(axis, half, rel, 1, 1, -1).start()
 
     begin(0)
     forward_first(0)
     pass_on(0, 3)
+    pass_on(0, 1)
     begin(1)
     ring_next(2)
-    pass_on(0, 1)
     forward_first(1)
     pass_on(1, 3)
     pass_on(1, 1)
     opposite(0)
     opposite(1)
     for rel in (0, 3, 1, 2):
-        for axis in both:
-            forward_second(axis, rel)
+        for half in both:
+            forward_second(half, rel)
         if rel == 3:
             ring_next(3)
-    for rel in (0, 3, 1, 2):
+    for half in both:
         for axis in both:
-            second(axis, rel, 2, 2, 1 if rel in (0, 1) else -1).wait_recv()
+            four = units.at[0:4, 0, 0, spans[axis][0] : spans[axis][2]]
+            pltpu.make_async_copy(four, four, ag_recv.at[axis, half, 8]).wait()
     ring_up(step(z, 4, 8), 3, False).wait_recv()
     ring_down(step(z, 4, 8), 3, False).wait_recv()
     to_mate(step(z, 4, 8), c, 1).start()
@@ -582,8 +593,10 @@
 
     swap.wait_send()
     for axis in both:
-        for k, sent in ((0, units.at[0:3, 0, 0]), (1, units.at[0:3, :, 0])):
-            pltpu.make_async_copy(sent, sent, ag_send.at[axis, k]).wait()
+        rows_ = slice(spans[axis][0], spans[axis][2])
+        for half in both:
+            for k, sent in ((0, units.at[0:3, 0, 0, rows_]), (1, units.at[0:3, :, 0, rows_])):
+                pltpu.make_async_copy(sent, sent, ag_send.at[axis, half, k]).wait()
     pltpu.make_async_copy(heads.at[0:7, 0], heads.at[0:7, 0], hd_send.at[0]).wait()
     pltpu.make_async_copy(heads.at[:, 0], heads.at[:, 0], hp_send.at[0]).wait()
 
@@ -597,10 +610,13 @@
         ts = jnp.sum(pieces[:, 1] * tk, axis=0, keepdims=True)
         tw = jnp.sum(pieces[:, 2] * tk, axis=0, keepdims=True)
         ss = jnp.sum(pieces[:, 4] * sk, axis=0, keepdims=True)
-        o_ref[cc : cc + 1, :] = tw / ts - tmax - jnp.log(ts) + smax + jnp.log(ss)
+        res[cc : cc + 1, :] = tw / ts - tmax - jnp.log(ts) + smax + jnp.log(ss)
 
     sent = out_rows.at[0, pl.ds(0, 62)]
+    cp_out = pltpu.make_async_copy(res, o_ref, load_sem.at[0])
+    cp_out.start()
     pltpu.make_async_copy(sent, sent, st_ssem.at[0]).wait()
+    cp_out.wait()
 
 
 def local(
@@ -609,12 +625,11 @@
 ):
     dma = pltpu.SemaphoreType.DMA
     vm = pltpu.VMEM
-    whole = pl.BlockSpec(memory_space=pltpu.VMEM)
     out = pl.pallas_call(
         kernel,
         out_shape=jax.ShapeDtypeStruct((2, 128), F32),
         in_specs=[pl.BlockSpec(memory_space=pl.ANY)] * 10,
-        out_specs=whole,
+        out_specs=pl.BlockSpec(memory_space=pl.ANY),
         scratch_shapes=[
             vm((3, 1, 256), jnp.int32),
             vm((2, 1, 256), F32),
@@ -638,14 +653,15 @@
             vm((2, 16, 8, 128), F32),
             vm((512, 768), BF),
             vm((4, 8, 128), F32),
-            dma((10,)),
+            vm((2, 128), F32),
+            dma((6,)),
             dma((2,)), dma((2,)),
             dma((2,)), dma((2,)),
             dma((1,)), dma((2, 6)),
             dma((1,)), dma((2, 6)),
             dma((2,)), dma((1,)),
             dma((1,)), dma((1,)),
-            dma((2, 2)), dma((2, 16)),
+            dma((2, 2, 2)), dma((2, 2, 9)),
             dma((1,)), dma((2, 4)),
             dma((1,)), dma((2,)),
             dma((1,)), dma((1,)),

time: 104 us -> 101 us (0.971)
  Pallas kernels: 102 us -> 99.4 us
    pallas_call x1, Pallas kernels: 102 us -> 99.4 us  [local(): pl.pallas_call(kernel, out_shape=jax.ShapeDtypeStruct((2, 128), F32), in_...]
where the time goes in v4:
time: 101 us
  Pallas kernels  99.4 us (98%)
  local copies, waits for them, and re-layouts  1.24 us (1%)
    pallas_call x1, Pallas kernels, local(): pl.pallas_call(kernel, out_shape=jax.ShapeDtypeStruct((2, 128), F32), in_...  99.4 us

profile of v4, /device:TPU:1, one launch (start us, length us, event | category | flops | bytes accessed | tf_op | source)
XLA Modules:
  0.0 100.7 jit_solution(1214373925505410570)
XLA Ops:
  0.0 99.4 %shard_map.100 = f32[2,128]{1,0:T(2,128)} custom-call(bf16[256,2048]{1,0:T(8,128)(2,1)} %tok_hbm.1, s32[1,256]{1,0:T(1,128)} %bitcast.8, s32[1,256]{1,0:T(1,128)} %bitcast.9, s32[1,256]{1,0:T(1,128)} %pr_hbm.1, bf16[1,2048,1024]{2,1,0:T(8,128)(2,1)} %win_hbm.1, bf16[1,1024,2048]{2,1,0:T(8,128)(2,1)} %wout_hbm.1, f32[1,2048]{1,0:T(1,128)} %bitcast.5, ...), custom_call_target="tpu_custom_call" | custom-call | tf_op jit(solution)/shard_map/pallas_call | solution.py:628
  99.4 1.2 %copy.12 = f32[256]{0:T(256)} copy(f32[256]{0:T(256)} %bitcast.7) | data formatting | bytes 2048

commit v5 on v4

--- a/solution.py
+++ b/solution.py
@@ -21,7 +21,7 @@
     o_ref,
     ids, gains,
     tok, out_rows, feats, w1, w2, acc, hid, part_send, part_recv, own_part, xin,
-    back, ret, unit, units, heads, st_send, st_recv, pick, factor, res,
+    back, ret, unit, units, heads, st_send, st_recv, pick, factor, res, square,
     load_sem, w_send, w_recv, disp_send, disp_recv, xag_send, xag_recv,
     rs_send, rs_recv, comb_send, comb_recv, pair_send, pair_recv,
     ag_send, ag_recv, hd_send, hd_recv, hp_send, hp_recv, st_ssem, st_rsem,
@@ -74,21 +74,45 @@
 
     barrier = pltpu.get_barrier_semaphore()
 
-    def greet(ee, vv):
-        @pl.when(jnp.logical_not((ee == e) & (vv == v)))
-        def _():
+    def greet(ee, vv, other):
+        def tell():
             pl.semaphore_signal(barrier, inc=1, device_id=(ee, vv), device_id_type=MESH)
 
-    def greet_rows(r, carry):
-        far = lax.rem(e + 16 + r, 32)
-        greet(far, x * 2 + home)
-        greet(c * 16 + lax.rem(e + r, 16), x * 2 + r // 16)
-        greet(z * 4 + r // 8, lax.rem(r, 8))
+        if other is None:
+            tell()
+        else:
+            pl.when(other)(tell)
+
+    far_first = [lax.rem(z + d, 8) for d in (4, 3, 5, 2, 6, 1, 7, 0)]
+    x0 = 2 * x
+    for k, zz in enumerate(far_first):
+
+        def greet_rows(r, carry):
+            ee = zz * 4 + lax.rem(y + 1 + r, 4)
+            greet(ee, x0 + home, None if k < 7 else (r < 3) | (home != c))
+            return carry
+
+        lax.fori_loop(0, 4, greet_rows, 0)
+
+        @pl.when(zz // 4 == c)
+        def _():
+            def greet_back(r, carry):
+                ee = zz * 4 + lax.rem(y + 1 + r, 4)
+                for cc in (0, 1):
+                    greet(ee, x0 + cc, None if k < 7 else (r < 3) | (cc != c))
+                return carry
+
+            lax.fori_loop(0, 4, greet_back, 0)
+
+    def greet_plane(r, carry):
+        for k in range(8):
+            vv = lax.rem(v + 1 + k, 8)
+            greet(z * 4 + lax.rem(y + 1 + r, 4), vv, None if k < 7 else r < 3)
         return carry
 
-    lax.fori_loop(0, 32, greet_rows, 0)
-    greet(step(z, 1, 8) * 4 + y, v)
-    greet(step(z, -1, 8) * 4 + y, v)
+    lax.fori_loop(0, 4, greet_plane, 0)
+    greet(step(z, 1, 8) * 4 + y, v, None)
+    greet(step(z, -1, 8) * 4 + y, v, None)
 
     cp_w1.start()
     pltpu.make_async_copy(ids, ids, load_sem.at[0]).wait()
@@ -127,8 +151,6 @@
 
     my_slot = pl.ds(3 * lax.rem(e, 16), 3)
 
-    far_first = [lax.rem(z + d, 8) for d in (4, 3, 5, 2, 6, 1, 7, 0)]
-
     def disp(to, h):
         return remote(
             out_rows.at[h, pl.ds(3 * to, 3)], feats.at[x, c, h, my_slot],
@@ -266,50 +288,59 @@
         cols = pl.ds(pl.multiple_of(xx * 512, 512), 512)
         return jnp.dot(hid[...], w2[:, cols], preferred_element_type=F32)
 
-    def rs(h, k, to):
+    def rs(q, k, to):
         return remote(
-            part_send.at[h, k], part_recv.at[h, k], rs_send.at[0], rs_recv.at[h, k],
+            part_send.at[q, k], part_recv.at[q, k], rs_send.at[0], rs_recv.at[q, min(k, 2)],
             at(z, y, to, c),
         )
 
+    quarters = range(4)
+
+    def far_sums(q):
+        rs(q, 0, xr).start()
+        rs(q, 1, xl).start()
+
     far = partial(xo).astype(BF)
-    for h in (0, 1):
-        part_send[h, 0] = far[:192, 256 * h : 256 * h + 256]
-        part_send[h, 1] = far[192:, 256 * h : 256 * h + 256]
-    rs(0, 0, xr).start()
-    rs(0, 1, xl).start()
+    for q in quarters:
+        part_send[q, 0] = far[:192, 128 * q : 128 * q + 128]
+        part_send[q, 1] = far[192:, 128 * q : 128 * q + 128]
+    far_sums(0)
     own_part[1] = partial(xr)
-    for h in (0, 1):
-        part_send[h, 2] = own_part[1, 192:, 256 * h : 256 * h + 256].astype(BF)
+    for q in quarters:
+        part_send[q, 2] = own_part[1, 192:, 128 * q : 128 * q + 128].astype(BF)
     rs(0, 2, xr).start()
     own_part[2] = partial(xl)
-    for h in (0, 1):
-        part_send[h, 3] = own_part[2, :192, 256 * h : 256 * h + 256].astype(BF)
+    for q in quarters:
+        part_send[q, 3] = own_part[2, :192, 128 * q : 128 * q + 128].astype(BF)
     rs(0, 3, xl).start()
 
-    def merge(h):
-        half = slice(256 * h, 256 * h + 256)
-        rs(h, 0, xr).wait_recv()
-        part_send[h, 4] = (own_part[1, :192, half] + part_recv[h, 0].astype(F32)).astype(BF)
-        rs(h, 4, xr).start()
-        rs(h, 1, xl).wait_recv()
-        part_send[h, 5] = (own_part[2, 192:, half] + part_recv[h, 1].astype(F32)).astype(BF)
-        rs(h, 5, xl).start()
-
-    merge(0)
-    rs(1, 0, xr).start()
-    rs(1, 1, xl).start()
-    rs(1, 2, xr).start()
-    rs(1, 3, xl).start()
-    own_part[0] = partial(x)
-
-    def comb(b, cc):
+    def near_sums(q):
+        rs(q, 2, xr).start()
+        rs(q, 3, xl).start()
+
+    def merge(q):
+        part = slice(128 * q, 128 * q + 128)
+        rs(q, 0, xr).wait_recv()
+        part_send[q, 4] = (own_part[1, :192, part] + part_recv[q, 0].astype(F32)).astype(BF)
+        rs(q, 4, xr).start()
+        rs(q, 1, xl).wait_recv()
+        part_send[q, 5] = (own_part[2, 192:, part] + part_recv[q, 1].astype(F32)).astype(BF)
+        rs(q, 5, xl).start()
+
+    def comb(b, q):
         return remote(
-            back.at[cc, pl.ds(3 * lax.rem(b, 16), 3)], ret.at[pl.ds(3 * e, 3)],
-            comb_send.at[cc], comb_recv.at[0], (b, x * 2 + cc),
+            back.at[q, pl.ds(3 * lax.rem(b, 16), 3)], ret.at[q % 2, pl.ds(3 * e, 3)],
+            comb_send.at[q], comb_recv.at[q % 2], (b, x * 2 + q // 2),
         )
 
-    def send_back(cc):
+    def send_back(q):
+        @pl.when((home == c) & (c == q // 2))
+        def _():
+            pltpu.make_async_copy(
+                back.at[q, pl.ds(3 * lax.rem(e, 16), 3)], ret.at[q % 2, pl.ds(3 * e, 3)],
+                comb_recv.at[q % 2],
+            ).start()
+
         for zz in far_first:
 
             @pl.when(zz // 4 == c)
@@ -317,166 +348,204 @@
                 def one(r, carry):
                     b = zz * 4 + lax.rem(y + 1 + r, 4)
 
-                    @pl.when(jnp.logical_not((b == e) & (cc == c)))
+                    @pl.when((b != e) | (c != q // 2))
                     def _():
-                        comb(b, cc).start()
+                        comb(b, q).start()
 
                     return carry
 
                 lax.fori_loop(0, 4, one, 0)
 
-    def collect(h):
-        half = slice(256 * h, 256 * h + 256)
+    def collect(q):
+        part = slice(128 * q, 128 * q + 128)
+        four = part_recv.at[q, 2:6]
+        pltpu.make_async_copy(four, four, rs_recv.at[q, 2]).wait()
         for rows_, near, merged in ((slice(0, 192), 3, 4), (slice(192, 384), 2, 5)):
-            rs(h, near, xr).wait_recv()
-            rs(h, merged, xr).wait_recv()
             total = (
-                own_part[0, rows_, half]
-                + part_recv[h, near].astype(F32)
-                + part_recv[h, merged].astype(F32)
+                own_part[0, rows_, part]
+                + part_recv[q, near].astype(F32)
+                + part_recv[q, merged].astype(F32)
             )
-            back[h, rows_.start // 8 : rows_.stop // 8] = total.reshape(24, 8, 256).astype(BF)
-        send_back(h)
-
+            back[q, rows_.start // 8 : rows_.stop // 8] = total.reshape(24, 8, 128).astype(BF)
+        send_back(q)
+
+    far_sums(1)
+    merge(0)
+    near_sums(1)
+    far_sums(2)
+    own_part[0] = partial(x)
+    merge(1)
     collect(0)
-    merge(1)
+    near_sums(2)
+    far_sums(3)
+    merge(2)
     collect(1)
-    cp_back = pltpu.make_async_copy(
-        back.at[c, pl.ds(3 * lax.rem(e, 16), 3)], ret.at[pl.ds(3 * e, 3)], comb_recv.at[0]
-    )
-
-    @pl.when(home == c)
-    def _():
-        cp_back.start()
-
-    swap = remote(
-        unit, units.at[y, x, c], pair_send.at[0], pair_recv.at[0], at(z, y, x, mate)
-    )
-    from_mate = remote(
-        unit, units.at[y, x, mate], pair_send.at[0], pair_recv.at[0], at(z, y, x, mate)
-    )
-
-    def finish(core):
-        pltpu.make_async_copy(ret, ret, comb_recv.at[0]).wait()
-        rows = ret[...].astype(F32).reshape(768, 256).astype(BF)
-        stream = tok[...].astype(F32)
-        kept = units.at[y, x, core]
+    near_sums(3)
+    merge(3)
+    collect(2)
+    collect(3)
+
+    def swap(sub):
+        return remote(
+            unit.at[sub, 0 : 256 + 16 * sub], units.at[y, x, 2 * c + sub, 0 : 256 + 16 * sub],
+            pair_send.at[sub], pair_recv.at[sub],
+            at(z, y, x, mate),
+        )
+
+    def finish(core, sub):
+        pltpu.make_async_copy(ret.at[sub], ret.at[sub], comb_recv.at[sub]).wait()
+        rows = ret[sub].astype(F32).reshape(768, 128).astype(BF)
+        part = slice(128 * sub, 128 * sub + 128)
+        stream = tok[:, part].astype(F32)
+        kept = units.at[y, x, 2 * core + sub]
+        given = unit.at[sub]
         squares = []
         for k in (0, 1):
             branch = jnp.dot(
                 pick[256 * k : 256 * k + 256], rows, preferred_element_type=F32
             )
             summed = stream + branch
-            scaled = (summed * gains[k]).astype(BF)
+            scaled = (summed * gains[k, :, part]).astype(BF)
             parts = (scaled[:128], scaled[128:])
             kept[128 * k : 128 * k + 128] = parts[core]
-            unit[128 * k : 128 * k + 128] = parts[1 - core]
+            given[128 * k : 128 * k + 128] = parts[1 - core]
             column = jnp.sum(summed * summed, axis=1, keepdims=True)
-            squares.append(jnp.broadcast_to(column, (256, 128)).T[:1])
-        low = lax.broadcasted_iota(jnp.int32, (16, 256), 0) == 0
-        for h, place in ((core, kept), (1 - core, unit)):
-            lines = []
+            row = jnp.broadcast_to(column, (256, 128)).T[:1]
+            if sub == 0:
+                square[k : k + 1] = row
+            else:
+                squares.append(row + square[k : k + 1])
+        if sub == 0:
+            swap(sub).start()
+            return
+        line_of = lax.broadcasted_iota(jnp.int32, (16, 128), 0)
+        for h, place in ((core, kept), (1 - core, given)):
+            table = jnp.zeros((16, 128), F32)
             for k in (0, 1):
-                part = squares[k][:, 128 * h : 128 * h + 128]
-                top = part.astype(BF).astype(F32)
-                lines.append(
-                    jnp.broadcast_to(jnp.concatenate([top, part - top], axis=1), (16, 256))
-                )
-            place[256:272] = jnp.where(low, lines[0], lines[1]).astype(BF)
-        swap.start()
+                total = squares[k][:, 128 * h : 128 * h + 128]
+                top = total.astype(BF).astype(F32)
+                for i, line in enumerate((top, total - top)):
+                    table = jnp.where(
+                        line_of == 2 * k + i, jnp.broadcast_to(line, (16, 128)), table
+                    )
+            place[256:272] = table.astype(BF)
+        swap(sub).start()
 
     here = (x, y)
-    spans = ((0, 64, 128), (128, 192, 272))
+    def span(axis, q):
+        if (axis + q) % 2 == 0:
+            return 0, 64, 128
+        return 128, 192, 272 if q % 2 else 256
+
 
     def dev_of(along, d):
         p, q = (step(x, d, 4), y) if along == 0 else (x, step(y, d, 4))
         return at(z, q, p, c)
 
-    def hop(axis, half, along, a, b, k, d, ends):
+    def hop(axis, q, along, a, b, group, d, ends):
         xx, yy = (a, b) if axis == 0 else (b, a)
-        piece = units.at[yy, xx, half, ends[0] : ends[1]]
+        piece = units.at[yy, xx, q, ends[0] : ends[1]]
         return remote(
-            piece, piece, ag_send.at[axis, half, min(k // 4, 1)], ag_recv.at[axis, half, k],
+            piece, piece, ag_send.at[q % 2, min(group // 2, 1)], ag_recv.at[axis, q, group],
             dev_of(along, d),
         )
 
-    def first(axis, half, k, off, d):
-        lo, mid, hi = spans[axis]
+    def first(axis, q, k, off, d):
+        lo, mid, hi = span(axis, q)
         ends = ((lo, hi), (lo, hi), (lo, mid), (mid, hi))[k]
         a = step(here[axis], off, 4)
-        return hop(axis, half, axis, a, here[1 - axis], k, d, ends)
-
-    def second(axis, half, rel, off, kind, d):
+        return hop(axis, q, axis, a, here[1 - axis], k // 2, d, ends)
+
+    def second(axis, q, rel, off, kind, d):
         a = step(here[axis], rel, 4)
         b = step(here[1 - axis], off, 4)
-        ends = (spans[axis][0], spans[axis][2])
-        return hop(axis, half, 1 - axis, a, b, 4 + (rel if kind == 0 else 4), d, ends)
+        lo, _, hi = span(axis, q)
+        ends = (lo, hi)
+        return hop(axis, q, 1 - axis, a, b, 2 + rel if kind == 0 else 6, d, ends)
+
+    def got(axis, q, group, count):
+        lo, _, hi = span(axis, q)
+        bulk = units.at[0:count, 0, 0, lo:hi]
+        pltpu.make_async_copy(bulk, bulk, ag_recv.at[axis, q, group]).wait()
 
     both = (0, 1)
 
-    def begin(half):
-        @pl.when(c == half)
-        def _():
-            finish(half)
-
-        @pl.when(c != half)
-        def _():
-            from_mate.wait_recv()
+    def begin(q):
+        @pl.when(c == q // 2)
+        def _():
+            finish(q // 2, q % 2)
+
+        @pl.when(c != q // 2)
+        def _():
+            swap(q % 2).wait_recv()
 
         for axis in both:
-            first(axis, half, 0, 0, 1).start()
-            first(axis, half, 1, 0, -1).start()
-        pass_on(half, 0)
-
-    def forward_first(half):
+            first(axis, q, 0, 0, 1).start()
+            first(axis, q, 1, 0, -1).start()
+        pass_on(q, 0)
+
+    def forward_first(q):
         for axis in both:
-            first(axis, half, 0, -1, 1).wait_recv()
-            first(axis, half, 2, -1, 1).start()
-            first(axis, half, 1, 1, -1).wait_recv()
-            first(axis, half, 3, 1, -1).start()
-
-    def pass_on(half, rel):
+            got(axis, q, 0, 2)
+            first(axis, q, 2, -1, 1).start()
+            first(axis, q, 3, 1, -1).start()
+
+    def pass_on(q, rel):
         for axis in both:
-            second(axis, half, rel, 0, 0, 1).start()
-            second(axis, half, rel, 0, 0, -1).start()
-
-    def opposite(half):
+            second(axis, q, rel, 0, 0, 1).start()
+            second(axis, q, rel, 0, 0, -1).start()
+
+    def opposite(q):
         for axis in both:
-            first(axis, half, 2, 2, 1).wait_recv()
-            first(axis, half, 3, 2, -1).wait_recv()
-        pass_on(half, 2)
-
-    def forward_second(half, rel):
+            got(axis, q, 1, 1)
+        pass_on(q, 2)
+
+    def forward_second(q, rel):
         for axis in both:
-            pair_of = units.at[0:2, 0, 0, spans[axis][0] : spans[axis][2]]
-            pltpu.make_async_copy(
-                pair_of, pair_of, ag_recv.at[axis, half, 4 + rel]
-            ).wait()
+            got(axis, q, 2 + rel, 2)
             if rel in (0, 1):
-                second(axis, half, rel, -1, 1, 1).start()
+                second(axis, q, rel, -1, 1, 1).start()
             else:
-                second(axis, half, rel, 1, 1, -1).start()
+                second(axis, q, rel, 1, 1, -1).start()
+
+    def spread_on(q):
+        forward_first(q)
+        pass_on(q, 3)
+        pass_on(q, 1)
 
     begin(0)
-    forward_first(0)
-    pass_on(0, 3)
-    pass_on(0, 1)
     begin(1)
+    spread_on(0)
+    begin(2)
     ring_next(2)
-    forward_first(1)
-    pass_on(1, 3)
-    pass_on(1, 1)
+    spread_on(1)
     opposite(0)
+    begin(3)
+    forward_second(0, 0)
+    spread_on(2)
     opposite(1)
-    for rel in (0, 3, 1, 2):
-        for half in both:
-            forward_second(half, rel)
-        if rel == 3:
-            ring_next(3)
-    for half in both:
+    forward_second(0, 3)
+    forward_second(1, 0)
+    forward_second(0, 1)
+    spread_on(3)
+    opposite(2)
+    forward_second(1, 3)
+    forward_second(0, 2)
+    forward_second(2, 0)
+    opposite(3)
+    forward_second(1, 1)
+    forward_second(1, 2)
+    ring_next(3)
+    forward_second(2, 3)
+    forward_second(3, 0)
+    forward_second(2, 1)
+    forward_second(3, 3)
+    forward_second(2, 2)
+    forward_second(3, 1)
+    forward_second(3, 2)
+    for q in quarters:
         for axis in both:
-            four = units.at[0:4, 0, 0, spans[axis][0] : spans[axis][2]]
-            pltpu.make_async_copy(four, four, ag_recv.at[axis, half, 8]).wait()
+            got(axis, q, 6, 4)
     ring_up(step(z, 4, 8), 3, False).wait_recv()
     ring_down(step(z, 4, 8), 3, False).wait_recv()
     to_mate(step(z, 4, 8), c, 1).start()
@@ -488,9 +557,9 @@
         for k in (0, 1):
             total = jnp.zeros((1, 128), F32)
             for xx in range(4):
-                for cc in (0, 1):
-                    line = units[yy, xx, cc, 256:272, :].astype(F32)[k : k + 1]
-                    total = total + line[:, :128] + line[:, 128:]
+                for q in (1, 3):
+                    lines = units[yy, xx, q, 256:272, :].astype(F32)
+                    total = total + lines[2 * k : 2 * k + 1] + lines[2 * k + 1 : 2 * k + 2]
             factor[yy, k : k + 1] = lax.rsqrt(total * (1.0 / 2048.0) + 1e-5)
 
     def logits(pair, k, n):
@@ -501,7 +570,13 @@
             for cc in (0, 1):
                 right = jnp.concatenate(
                     [
-                        units[2 * pair + i, xx, cc, 128 * k : 128 * k + 128, :]
+                        jnp.concatenate(
+                            [
+                                units[2 * pair + i, xx, 2 * cc + h, 128 * k : 128 * k + 128, :]
+                                for h in (0, 1)
+                            ],
+                            axis=1,
+                        )
                         for i in (0, 1)
                     ],
                     axis=0,
@@ -548,19 +623,21 @@
 
     me = 4 * y + x
 
-    def st_copy(r):
-        yy = lax.rem(y + r // 8, 4)
-        vv = lax.rem(v + lax.rem(r, 8), 8)
-        return remote(
-            st_send.at[yy], st_recv.at[c, me], st_ssem.at[0], st_rsem.at[0],
-            (z * 4 + yy, vv),
-        )
-
-    def send_stats(r, carry):
-        st_copy(r).start()
-        return carry
-
-    lax.fori_loop(1, 32, send_stats, 0)
+    for dy in (2, 1, 3, 0):
+        yy = step(y, dy, 4)
+
+        def send_stats(r, carry):
+            remote(
+                st_send.at[yy], st_recv.at[c, me], st_ssem.at[0], st_rsem.at[0],
+                (z * 4 + yy, lax.rem(v + 3 + r, 8)),
+            ).start()
+            return carry
+
+        if dy:
+            lax.fori_loop(0, 8, send_stats, 0)
+        else:
+            lax.fori_loop(0, 5, send_stats, 0)
+            lax.fori_loop(6, 8, send_stats, 0)
     pltpu.make_async_copy(st_send.at[y], st_recv.at[c, me], st_rsem.at[0]).start()
 
     rw1.wait_send()
@@ -580,23 +657,25 @@
     pltpu.make_async_copy(feats.at[0:3], feats.at[0:3], xag_send.at[0]).wait()
     pltpu.make_async_copy(part_send, part_send, rs_send.at[0]).wait()
 
-    for h in (0, 1):
-
-        @pl.when((home == c) & (c == h))
-        def _():
-            most = back.at[h, pl.ds(0, 45)]
-            pltpu.make_async_copy(most, most, comb_send.at[h]).wait()
-
-        @pl.when(jnp.logical_not((home == c) & (c == h)))
-        def _():
-            pltpu.make_async_copy(back.at[h], back.at[h], comb_send.at[h]).wait()
-
-    swap.wait_send()
-    for axis in both:
-        rows_ = slice(spans[axis][0], spans[axis][2])
-        for half in both:
-            for k, sent in ((0, units.at[0:3, 0, 0, rows_]), (1, units.at[0:3, :, 0, rows_])):
-                pltpu.make_async_copy(sent, sent, ag_send.at[axis, half, k]).wait()
+    for q in quarters:
+
+        @pl.when((home == c) & (c == q // 2))
+        def _():
+            most = back.at[q, pl.ds(0, 45)]
+            pltpu.make_async_copy(most, most, comb_send.at[q]).wait()
+
+        @pl.when(jnp.logical_not((home == c) & (c == q // 2)))
+        def _():
+            pltpu.make_async_copy(back.at[q], back.at[q], comb_send.at[q]).wait()
+
+    for sub in (0, 1):
+        swap(sub).wait_send()
+    for sub, rows_ in ((0, 256), (1, 272)):
+        for k, sent in (
+            (0, units.at[0:3, 0, 0:2, 0:rows_]),
+            (1, units.at[0:3, :, 0:2, 0:rows_]),
+        ):
+            pltpu.make_async_copy(sent, sent, ag_send.at[sub, k]).wait()
     pltpu.make_async_copy(heads.at[0:7, 0], heads.at[0:7, 0], hd_send.at[0]).wait()
     pltpu.make_async_copy(heads.at[:, 0], heads.at[:, 0], hp_send.at[0]).wait()
 
@@ -640,28 +719,29 @@
             vm((2048, 2048), BF),
             vm((2, 384, 1024), F32),
             vm((384, 2048), BF),
-            vm((2, 6, 192, 256), BF),
-            vm((2, 6, 192, 256), BF),
+            vm((4, 6, 192, 128), BF),
+            vm((4, 6, 192, 128), BF),
             vm((3, 384, 512), F32),
             vm((4, 384, 512), BF),
-            vm((2, 48, 8, 256), BF),
-            vm((96, 8, 256), BF),
-            vm((272, 256), BF),
-            vm((4, 4, 2, 272, 256), BF),
+            vm((4, 48, 8, 128), BF),
+            vm((2, 96, 8, 128), BF),
+            vm((2, 272, 128), BF),
+            vm((4, 4, 4, 272, 128), BF),
             vm((8, 2, 2, 64, 2048), BF),
             vm((4, 8, 128), F32),
             vm((2, 16, 8, 128), F32),
             vm((512, 768), BF),
             vm((4, 8, 128), F32),
             vm((2, 128), F32),
+            vm((8, 256), F32),
             dma((6,)),
             dma((2,)), dma((2,)),
             dma((2,)), dma((2,)),
             dma((1,)), dma((2, 6)),
-            dma((1,)), dma((2, 6)),
-            dma((2,)), dma((1,)),
-            dma((1,)), dma((1,)),
-            dma((2, 2, 2)), dma((2, 2, 9)),
+            dma((1,)), dma((4, 3)),
+            dma((4,)), dma((2,)),
+            dma((2,)), dma((2,)),
+            dma((2, 2)), dma((2, 4, 7)),
             dma((1,)), dma((2, 4)),
             dma((1,)), dma((2,)),
             dma((1,)), dma((1,)),

time: 101 us -> 98.3 us (0.973)
  Pallas kernels: 99.4 us -> 97 us
    pallas_call x1, Pallas kernels: 99.4 us -> 97 us  [local(): pl.pallas_call(kernel, out_shape=jax.ShapeDtypeStruct((2, 128), F32), in_...]
where the time goes in v5:
time: 98.3 us; the launch traced here: 98.2 us
  Pallas kernels  97 us (99%)
  local copies, waits for them, and re-layouts  1.24 us (1%)
    pallas_call x1, Pallas kernels, local(): pl.pallas_call(kernel, out_shape=jax.ShapeDtypeStruct((2, 128), F32), in_...  97 us

profile of v5, /device:TPU:1, one launch (start us, length us, event | category | flops | bytes accessed | tf_op | source)
XLA Modules:
  0.0 98.2 jit_solution(17405357049728179427)
XLA Ops:
  0.0 97.0 %shard_map.100 = f32[2,128]{1,0:T(2,128)} custom-call(bf16[256,2048]{1,0:T(8,128)(2,1)} %tok_hbm.1, s32[1,256]{1,0:T(1,128)} %bitcast.8, s32[1,256]{1,0:T(1,128)} %bitcast.9, s32[1,256]{1,0:T(1,128)} %pr_hbm.1, bf16[1,2048,1024]{2,1,0:T(8,128)(2,1)} %win_hbm.1, bf16[1,1024,2048]{2,1,0:T(8,128)(2,1)} %wout_hbm.1, f32[1,2048]{1,0:T(1,128)} %bitcast.5, ...), custom_call_target="tpu_custom_call" | custom-call | tf_op jit(solution)/shard_map/pallas_call | solution.py:707
  97.0 1.2 %copy.12 = f32[256]{0:T(256)} copy(f32[256]{0:T(256)} %bitcast.7) | data formatting | bytes 2048

commit v6 on v5

--- a/solution.py
+++ b/solution.py
@@ -544,23 +544,19 @@
     forward_second(3, 1)
     forward_second(3, 2)
     for q in quarters:
-        for axis in both:
-            got(axis, q, 6, 4)
-    ring_up(step(z, 4, 8), 3, False).wait_recv()
-    ring_down(step(z, 4, 8), 3, False).wait_recv()
-    to_mate(step(z, 4, 8), c, 1).start()
-
+        got(1, q, 6, 4)
     def from_mate_heads(k):
         pltpu.make_async_copy(heads.at[0:4, 0], heads.at[0:4, 0], hp_recv.at[k]).wait()
 
-    for yy in range(4):
-        for k in (0, 1):
-            total = jnp.zeros((1, 128), F32)
-            for xx in range(4):
-                for q in (1, 3):
-                    lines = units[yy, xx, q, 256:272, :].astype(F32)
-                    total = total + lines[2 * k : 2 * k + 1] + lines[2 * k + 1 : 2 * k + 2]
-            factor[yy, k : k + 1] = lax.rsqrt(total * (1.0 / 2048.0) + 1e-5)
+    def factors(pair):
+        for i in (0, 1):
+            for k in (0, 1):
+                total = jnp.zeros((1, 128), F32)
+                for xx in range(4):
+                    for q in (1, 3):
+                        lines = units[2 * pair + i, xx, q, 256:272, :].astype(F32)
+                        total = total + lines[2 * k : 2 * k + 1] + lines[2 * k + 1 : 2 * k + 2]
+                factor[2 * pair + i, k : k + 1] = lax.rsqrt(total * (1.0 / 2048.0) + 1e-5)
 
     def logits(pair, k, n):
         left = [heads[lax.rem(z + 4 * n + i, 8), :, k].reshape(128, 2048) for i in range(4)]
@@ -589,37 +585,48 @@
         scale = [factor[2 * pair + i, k : k + 1] for i in (0, 1)]
         return total * jnp.concatenate(scale, axis=1)
 
-    def chunk(n):
-        def one_pair(pair, carry):
-            tl = logits(pair, 0, n)
-            sl = logits(pair, 1, n)
-            tm = jnp.max(tl, axis=0, keepdims=True)
-            sm = jnp.max(sl, axis=0, keepdims=True)
-            if n == 1:
-                old = jnp.concatenate([st_send[2 * pair], st_send[2 * pair + 1]], axis=1)
-                tm = jnp.maximum(tm, old[0:1])
-                sm = jnp.maximum(sm, old[3:4])
-            te = jnp.exp(tl - tm)
-            ts = jnp.sum(te, axis=0, keepdims=True)
-            tw = jnp.sum(te * (tl - sl), axis=0, keepdims=True)
-            ss = jnp.sum(jnp.exp(sl - sm), axis=0, keepdims=True)
-            if n == 1:
-                keep = jnp.exp(old[0:1] - tm)
-                ts = ts + old[1:2] * keep
-                tw = tw + old[2:3] * keep
-                ss = ss + old[4:5] * jnp.exp(old[3:4] - sm)
-            zero = jnp.zeros((3, 256), F32)
-            table = jnp.concatenate([tm, ts, tw, sm, ss, zero], axis=0)
-            st_send[2 * pair] = table[:, :128]
-            st_send[2 * pair + 1] = table[:, 128:]
-            return carry
-
-        lax.fori_loop(0, 2, one_pair, 0)
-
+    def one_pair(pair, n):
+        tl = logits(pair, 0, n)
+        sl = logits(pair, 1, n)
+        tm = jnp.max(tl, axis=0, keepdims=True)
+        sm = jnp.max(sl, axis=0, keepdims=True)
+        if n == 1:
+            old = jnp.concatenate([st_send[2 * pair], st_send[2 * pair + 1]], axis=1)
+            tm = jnp.maximum(tm, old[0:1])
+            sm = jnp.maximum(sm, old[3:4])
+        te = jnp.exp(tl - tm)
+        ts = jnp.sum(te, axis=0, keepdims=True)
+        tw = jnp.sum(te * (tl - sl), axis=0, keepdims=True)
+        ss = jnp.sum(jnp.exp(sl - sm), axis=0, keepdims=True)
+        if n == 1:
+            keep = jnp.exp(old[0:1] - tm)
+            ts = ts + old[1:2] * keep
+            tw = tw + old[2:3] * keep
+            ss = ss + old[4:5] * jnp.exp(old[3:4] - sm)
+        zero = jnp.zeros((3, 256), F32)
+        table = jnp.concatenate([tm, ts, tw, sm, ss, zero], axis=0)
+        st_send[2 * pair] = table[:, :128]
+        st_send[2 * pair + 1] = table[:, 128:]
+
+    near_pair = y // 2
     from_mate_heads(0)
-    chunk(0)
+    factors(near_pair)
+    one_pair(near_pair, 0)
+    for q in quarters:
+        got(0, q, 6, 4)
+    for k, arrived in enumerate((ring_up, ring_down)):
+        arrived(step(z, 4, 8), 3, False).wait_recv()
+        piece = heads.at[step(z, 4, 8), c, k]
+        remote(piece, piece, hp_send.at[0], hp_recv.at[1], at(z, y, x, mate)).start()
+    factors(1 - near_pair)
+    one_pair(1 - near_pair, 0)
     from_mate_heads(1)
-    chunk(1)
+
+    def second_chunk(pair, carry):
+        one_pair(pair, 1)
+        return carry
+
+    lax.fori_loop(0, 2, second_chunk, 0)
 
     me = 4 * y + x
 

time: 98.3 us -> 98.4 us (level)
  no operation moved by 1% of the time
where the time goes in v6:
time: 98.4 us; the launch traced here: 98.3 us
  Pallas kernels  97 us (99%)
  local copies, waits for them, and re-layouts  1.24 us (1%)
    pallas_call x1, Pallas kernels, local(): pl.pallas_call(kernel, out_shape=jax.ShapeDtypeStruct((2, 128), F32), in_...  97 us

profile of v6, /device:TPU:1, one launch (start us, length us, event | category | flops | bytes accessed | tf_op | source)
XLA Modules:
  0.0 98.3 jit_solution(13509981507126855581)
XLA Ops:
  0.0 97.0 %shard_map.100 = f32[2,128]{1,0:T(2,128)} custom-call(bf16[256,2048]{1,0:T(8,128)(2,1)} %tok_hbm.1, s32[1,256]{1,0:T(1,128)} %bitcast.8, s32[1,256]{1,0:T(1,128)} %bitcast.9, s32[1,256]{1,0:T(1,128)} %pr_hbm.1, bf16[1,2048,1024]{2,1,0:T(8,128)(2,1)} %win_hbm.1, bf16[1,1024,2048]{2,1,0:T(8,128)(2,1)} %wout_hbm.1, f32[1,2048]{1,0:T(1,128)} %bitcast.5, ...), custom_call_target="tpu_custom_call" | custom-call | tf_op jit(solution)/shard_map/pallas_call | solution.py:714
  97.0 1.2 %copy.12 = f32[256]{0:T(256)} copy(f32[256]{0:T(256)} %bitcast.7) | data formatting | bytes 2048
